TPU v7x, 32 devices: a whole 2x2x4 slice. The times are simulated.
32 devices in a mesh: stream: 4 (over y, x), replica: 8 (over z, core).
Axes of the slice: x: 2, y: 2, z: 4, core: 2. Of those that a mesh axis runs over, the one named last changes fastest.
Arguments:
- query_embeds: bfloat16 [64, 32, 384], P(('stream', 'replica')), may hold values from -6 to 6
- doc_embeds: bfloat16 [32, 512, 384], P(('stream', 'replica')), may hold values from -6 to 6
- doc_segments: int32 [32, 512], P(('stream', 'replica')), may hold values from 0 to 3, never falling along the last dimension, each value on 1 to 256 neighbouring positions
- candidates: int32 [64, 16], replicated, may hold values from 0 to 127, all different within a row; in each aligned block of 64 rows (0 to 63, 64 to 127, ...) at most 32 rows name the same one
- neg_counts: int32 [64], replicated, may hold values from 1 to 15
- w_qkv: float32 [384, 1152], replicated, may hold values from -0.3125 to 0.3125
- w_out: float32 [384, 384], replicated, may hold values from -1.25 to 1.25
- w_up: float32 [384, 1536], replicated, may hold values from -0.3125 to 0.3125
- w_down: float32 [1536, 384], replicated, may hold values from -0.15625 to 0.15625
- w_head: float32 [384, 96], replicated, may hold values from -0.3125 to 0.3125
- vectors: float32 [5088], replicated, may hold values from -2 to 2, as said below
- mom_qkv: float32 [384, 1152], replicated, may hold values from -6 to 6
- mom_out: float32 [384, 384], replicated, may hold values from -6 to 6
- mom_up: float32 [384, 1536], replicated, may hold values from -6 to 6
- mom_down: float32 [1536, 384], replicated, may hold values from -6 to 6
- mom_head: float32 [384, 96], replicated, may hold values from -6 to 6
- mom_vectors: float32 [5088], replicated, may hold values from -6 to 6
- err_qkv: float32 [8, 384, 1152], P('replica'), may hold values from -3.5 to 3.5
- err_out: float32 [8, 384, 384], P('replica'), may hold values from -3.5 to 3.5
- err_up: float32 [8, 384, 1536], P('replica'), may hold values from -3.5 to 3.5
- err_down: float32 [8, 1536, 384], P('replica'), may hold values from -3.5 to 3.5
- err_head: float32 [8, 384, 96], P('replica'), may hold values from -3.5 to 3.5
- fac_qkv: float32 [1152, 8], replicated, may hold values from -6 to 6
- fac_out: float32 [384, 8], replicated, may hold values from -6 to 6
- fac_up: float32 [1536, 8], replicated, may hold values from -6 to 6
- fac_down: float32 [384, 8], replicated, may hold values from -6 to 6
- fac_head: float32 [96, 8], replicated, may hold values from -6 to 6
Outputs:
- loss: float32 [], replicated
- new_qkv: float32 [384, 1152], replicated
- new_out: float32 [384, 384], replicated
- new_up: float32 [384, 1536], replicated
- new_down: float32 [1536, 384], replicated
- new_head: float32 [384, 96], replicated
- new_vectors: float32 [5088], replicated
- newmom_qkv: float32 [384, 1152], replicated
- newmom_out: float32 [384, 384], replicated
- newmom_up: float32 [384, 1536], replicated
- newmom_down: float32 [1536, 384], replicated
- newmom_head: float32 [384, 96], replicated
- newmom_vectors: float32 [5088], replicated
- newerr_qkv: float32 [8, 384, 1152], P('replica')
- newerr_out: float32 [8, 384, 384], P('replica')
- newerr_up: float32 [8, 384, 1536], P('replica')
- newerr_down: float32 [8, 1536, 384], P('replica')
- newerr_head: float32 [8, 384, 96], P('replica')
- newfac_qkv: float32 [1152, 8], replicated
- newfac_out: float32 [384, 8], replicated
- newfac_up: float32 [1536, 8], replicated
- newfac_down: float32 [384, 8], replicated
- newfac_head: float32 [96, 8], replicated
Inputs may be any that keep to these rules, and one draw needn't show every extreme that they name: `doc_segments`: each row holds all 4 documents in order, each 1 to 256 tokens, one of exactly 256. `candidates`: A query's 16 ids are distinct; no document is named by more than 32 queries, a bound that some block reaches. `vectors`: gains lie near one, biases near zero.
All inputs are finite; a program needn't handle non-finite values.
Results may differ from a plain program's by a relative error of at most 0.0004.
Values may be sent and summed in bfloat16 or wider, within the bound.
No kernel may reach another device: no remote copies, remote signals or barrier semaphores. Data moves between devices by JAX's collectives and lax.ppermute only.
A program may use at most 192 MiB of HBM per device.

v0:
```python
import math

import jax
import jax.numpy as jnp
import numpy as np
from jax import lax
from jax.experimental import pallas as pl
from jax.experimental.pallas import tpu as pltpu
from jax.sharding import PartitionSpec as P

D = 384
HEADS = 12
HDIM = 32
FF = 1536
NSEG = 4


HIGH = lax.Precision.HIGHEST
SOFT = 0.03
MOMENTUM = 0.9
RATE = 0.1


def split_vec(packed):
    return jnp.split(
        packed,
        [3 * D, 4 * D, 4 * D + FF, 5 * D + FF, 6 * D + FF, 7 * D + FF, 8 * D + FF, 9 * D + FF],
    )


def inner(first, second):
    return lax.dot_general(
        first, second, (((0,), (0,)), ((), ())), preferred_element_type=jnp.float32
    )


def layer_norm(resid, gain, shift):
    center = resid - jnp.mean(resid, -1, keepdims=True)
    inv_std = lax.rsqrt(jnp.mean(center * center, -1, keepdims=True) + 1e-05)
    normed = center * inv_std
    return (normed * gain + shift, normed, inv_std)


def norm_back(grad_out, gain, normed, inv_std):
    scaled = grad_out * gain
    grad_in = inv_std * (
        scaled
        - jnp.mean(scaled, -1, keepdims=True)
        - normed * jnp.mean(scaled * normed, -1, keepdims=True)
    )
    return (grad_in, jnp.sum(grad_out * normed, 0), jnp.sum(grad_out, 0))


def gelu(value):
    return 0.5 * value * (1.0 + jax.scipy.special.erf(value * 0.7071067811865476))


def gelu_slope(value):
    return (
        0.5 * (1.0 + jax.scipy.special.erf(value * 0.7071067811865476))
        + value * jnp.exp(-0.5 * value * value) * 0.3989422804014327
    )


def rotary(value, cosine, sine):
    half = value.shape[-1] // 2
    return value * cosine + jnp.concatenate([-value[..., half:], value[..., :half]], -1) * sine


def rotary_back(grad, cosine, sine):
    half = grad.shape[-1] // 2
    turned = grad * sine
    return grad * cosine + jnp.concatenate([turned[..., half:], -turned[..., :half]], -1)


def tables(segment):
    count = segment.shape[0]
    places = jnp.arange(count)
    same = segment[:, None] == segment[None, :]
    position = jnp.sum(same & (places[None, :] < places[:, None]), 1).astype(jnp.float32)
    freqs = 10000.0 ** (-(jnp.arange(HDIM // 2).astype(jnp.float32) * 2.0) / HDIM)
    angle = position[:, None] * freqs[None, :]
    cosine = jnp.concatenate([jnp.cos(angle), jnp.cos(angle)], -1)[:, None, :]
    sine = jnp.concatenate([jnp.sin(angle), jnp.sin(angle)], -1)[:, None, :]
    return (same, cosine, sine)


def encode(tokens_in, same, cosine, sine, mats, packed):
    w_qkv, w_out, w_up, w_down, w_head = mats
    b_qkv, b_out, b_up, b_down, gain_one, shift_one, gain_two, shift_two, b_head = split_vec(packed)
    count = tokens_in.shape[0]
    scale = HDIM ** (-0.5)
    qkv = (jnp.dot(tokens_in, w_qkv, preferred_element_type=jnp.float32) + b_qkv).reshape(
        count, 3, HEADS, HDIM
    )
    queries = rotary(qkv[:, 0], cosine, sine).astype(jnp.bfloat16)
    keys_rot = rotary(qkv[:, 1], cosine, sine).astype(jnp.bfloat16)
    values = qkv[:, 2].astype(jnp.bfloat16)
    scores = (
        jnp.einsum("ihd,jhd->hij", queries, keys_rot, preferred_element_type=jnp.float32) * scale
    )
    scores = jnp.where(same[None], scores, -1e30)
    expo = jnp.exp(scores - jnp.max(scores, -1, keepdims=True))
    probs = expo / jnp.sum(expo, -1, keepdims=True)
    probs_low = probs.astype(jnp.bfloat16)
    context = (
        jnp.einsum("hij,jhd->ihd", probs_low, values, preferred_element_type=jnp.float32)
        .reshape(count, D)
        .astype(jnp.bfloat16)
    )
    attended = jnp.dot(context, w_out, preferred_element_type=jnp.float32) + b_out
    hidden_one, normed_one, inv_one = layer_norm(
        tokens_in.astype(jnp.float32) + attended, gain_one, shift_one
    )
    hidden_low = hidden_one.astype(jnp.bfloat16)
    pre_act = jnp.dot(hidden_low, w_up, preferred_element_type=jnp.float32) + b_up
    act_low = gelu(pre_act).astype(jnp.bfloat16)
    mixed = jnp.dot(act_low, w_down, preferred_element_type=jnp.float32) + b_down
    hidden_two, normed_two, inv_two = layer_norm(hidden_one + mixed, gain_two, shift_two)
    second_low = hidden_two.astype(jnp.bfloat16)
    emitted = jnp.dot(second_low, w_head, preferred_element_type=jnp.float32) + b_head
    inv_len = lax.rsqrt(jnp.sum(emitted * emitted, -1, keepdims=True) + 1e-06)
    output = emitted * inv_len
    kept = (
        queries,
        keys_rot,
        values,
        probs,
        probs_low,
        context,
        normed_one,
        inv_one,
        hidden_low,
        pre_act,
        act_low,
        normed_two,
        inv_two,
        second_low,
        inv_len,
        output,
    )
    return (output, kept)


def backward(grad_vec, tokens_in, cosine, sine, kept, mats, packed):
    w_qkv, w_out, w_up, w_down, w_head = mats
    b_qkv, b_out, b_up, b_down, gain_one, shift_one, gain_two, shift_two, b_head = split_vec(packed)
    (
        queries,
        keys_rot,
        values,
        probs,
        probs_low,
        context,
        normed_one,
        inv_one,
        hidden_low,
        pre_act,
        act_low,
        normed_two,
        inv_two,
        second_low,
        inv_len,
        output,
    ) = kept
    count = tokens_in.shape[0]
    scale = HDIM ** (-0.5)
    grad_emit = inv_len * (grad_vec - output * jnp.sum(grad_vec * output, -1, keepdims=True))
    emit_low = grad_emit.astype(jnp.bfloat16)
    grad_hidden_two = jnp.dot(emit_low, w_head.T, preferred_element_type=jnp.float32)
    grad_resid_two, grad_gain_two, grad_shift_two = norm_back(
        grad_hidden_two, gain_two, normed_two, inv_two
    )
    mixed_low = grad_resid_two.astype(jnp.bfloat16)
    grad_act = jnp.dot(mixed_low, w_down.T, preferred_element_type=jnp.float32)
    grad_pre = grad_act * gelu_slope(pre_act)
    pre_low = grad_pre.astype(jnp.bfloat16)
    grad_hidden_one = grad_resid_two + jnp.dot(pre_low, w_up.T, preferred_element_type=jnp.float32)
    grad_resid_one, grad_gain_one, grad_shift_one = norm_back(
        grad_hidden_one, gain_one, normed_one, inv_one
    )
    attn_low = grad_resid_one.astype(jnp.bfloat16)
    grad_context = (
        jnp.dot(attn_low, w_out.T, preferred_element_type=jnp.float32)
        .reshape(count, HEADS, HDIM)
        .astype(jnp.bfloat16)
    )
    grad_probs = jnp.einsum(
        "ihd,jhd->hij", grad_context, values, preferred_element_type=jnp.float32
    )
    grad_values = jnp.einsum(
        "hij,ihd->jhd", probs_low, grad_context, preferred_element_type=jnp.float32
    )
    grad_scores = probs * (grad_probs - jnp.sum(grad_probs * probs, -1, keepdims=True))
    scores_low = grad_scores.astype(jnp.bfloat16)
    grad_queries = (
        jnp.einsum("hij,jhd->ihd", scores_low, keys_rot, preferred_element_type=jnp.float32) * scale
    )
    grad_keys = (
        jnp.einsum("hij,ihd->jhd", scores_low, queries, preferred_element_type=jnp.float32) * scale
    )
    grad_queries = rotary_back(grad_queries, cosine, sine)
    grad_keys = rotary_back(grad_keys, cosine, sine)
    grad_qkv_act = jnp.stack([grad_queries, grad_keys, grad_values], 1).reshape(count, 3 * D)
    grad_packed = jnp.concatenate(
        [
            jnp.sum(grad_qkv_act, 0),
            jnp.sum(grad_resid_one, 0),
            jnp.sum(grad_pre, 0),
            jnp.sum(grad_resid_two, 0),
            grad_gain_one,
            grad_shift_one,
            grad_gain_two,
            grad_shift_two,
            jnp.sum(grad_emit, 0),
        ]
    )
    pairs = (
        (tokens_in, grad_qkv_act.astype(jnp.bfloat16)),
        (context, attn_low),
        (hidden_low, pre_low),
        (act_low, mixed_low),
        (second_low, emit_low),
    )
    return (pairs, grad_packed)


AXES = ("stream", "replica")


def spread(value, devices):
    copies = jnp.broadcast_to(value[None], (devices,) + value.shape)
    return lax.all_to_all(copies, AXES, 0, 0, tiled=True)


def all_sum(value):
    count = lax.axis_size("stream") * lax.axis_size("replica")
    rows, cols = value.shape
    pieces = value.reshape(rows, count, cols // count).transpose(1, 0, 2)
    got = lax.all_to_all(pieces, AXES, 0, 0, tiled=True)
    mine = jnp.sum(got, 0)
    back = spread(mine, count)
    return back.transpose(1, 0, 2).reshape(rows, cols)


def thirds(value):
    high = lax.reduce_precision(value, 8, 7)
    rest = value - high
    mid = lax.reduce_precision(rest, 8, 7)
    low = rest - mid
    return [part.astype(jnp.bfloat16) for part in (high, mid, low)]


def basis_kernel(bounds, left_ref, out_ref):
    blocks = [left_ref[:, lo:hi] for lo, hi in bounds]
    places = lax.broadcasted_iota(jnp.int32, (8, 1), 0)
    for turn in range(8):
        for n, block in enumerate(blocks):
            row = block[turn : turn + 1]
            row = row * lax.rsqrt(jnp.sum(row * row, -1, keepdims=True) + 1e-12)
            shares = jnp.sum(block * row, -1, keepdims=True)
            shares = jnp.where(places > turn, shares, 0.0)
            block = block - shares * row
            blocks[n] = jnp.where(places == turn, row, block)
    for (lo, hi), block in zip(bounds, blocks):
        out_ref[:, lo:hi] = block


def split_rows(value):
    high = value.astype(jnp.bfloat16)
    rest = value - high.astype(jnp.float32)
    mid = rest.astype(jnp.bfloat16)
    low = (rest - mid.astype(jnp.float32)).astype(jnp.bfloat16)
    return [high, mid, low]


def matmul(left, right, contract):
    return lax.dot_general(left, right, (contract, ((), ())), preferred_element_type=jnp.float32)


NN, NT, TN = ((1,), (0,)), ((1,), (1,)), ((0,), (0,))


SPOTS = (0, 3 * D, 4 * D, 4 * D + FF, 5 * D + FF, 6 * D + FF, 7 * D + FF, 8 * D + FF, 9 * D + FF)
SCALE = HDIM ** (-0.5)
TILE = 512


def turn_table():
    freqs = (10000.0 ** (-(np.arange(HDIM // 2).astype(np.float32) * 2.0) / HDIM)).astype(np.float32)
    angle = np.arange(256, dtype=np.float32)[:, None] * freqs[None, :]
    wide = np.concatenate([np.tile(np.cos(angle), 8), np.tile(np.sin(angle), 8)], 1)
    rest = wide.astype(np.float32)
    parts = []
    for _ in range(3):
        part = rest.astype(jnp.bfloat16)
        parts.append(part)
        rest = rest - part.astype(np.float32)
    return np.concatenate(parts, 1)


def lanes(shape):
    return lax.broadcasted_iota(jnp.int32, shape, 1)


def turned(value, cosine, sine, sign):
    first = (lanes(value.shape) % HDIM) < HDIM // 2
    if sign > 0:
        rot = jnp.where(first, -pltpu.roll(value, 112, 1), pltpu.roll(value, 16, 1))
        return value * cosine + rot * sine
    part = value * sine
    return value * cosine + jnp.where(first, pltpu.roll(part, 112, 1), -pltpu.roll(part, 16, 1))


def head_mask(head, rows):
    return (lanes((rows, 128)) // HDIM) == head


def bias(vec_ref, n, width):
    return vec_ref[:, SPOTS[n] : SPOTS[n] + width]


def norm(resid):
    center = resid - jnp.mean(resid, -1, keepdims=True)
    inv_std = lax.rsqrt(jnp.mean(center * center, -1, keepdims=True) + 1e-05)
    return center * inv_std, inv_std


def encode_kernel(first, *refs):
    x_ref, segc_ref, segr_ref, table_ref = refs[:4]
    weights, vec_ref = refs[4:9], refs[9]
    (
        q_ref, k_ref, v_ref, ctx_ref, n1_ref, h1_ref, pre_ref, act_ref, n2_ref, h2_ref, out_ref,
        low_ref, stat_ref, cos_ref, sin_ref,
    ) = refs[10:25]
    if first:
        for w_ref, low in zip(weights, refs[25:30]):
            low[...] = w_ref[...].astype(jnp.bfloat16)
        weights = refs[25:30]
    wqkv_ref, wout_ref, wup_ref, wdown_ref, whead_ref = weights
    count = x_ref.shape[0]
    tile = min(count, TILE)
    starts = [
        jnp.sum((segr_ref[...] < d).astype(jnp.int32), -1, keepdims=True) for d in range(NSEG)
    ]

    def project(t, _):
        rows = pl.ds(pl.multiple_of(t * tile, tile), tile)
        place = t * tile + lax.broadcasted_iota(jnp.int32, (tile, 1), 0)
        for d in range(NSEG):
            place = jnp.where(segc_ref[rows, :] == d, place - starts[d], place)
        hot = (place == lanes((tile, 256))).astype(jnp.float32).astype(jnp.bfloat16)
        both = matmul(hot, table_ref[...], NN)
        both = both[:, :256] + both[:, 256:512] + both[:, 512:]
        cosine, sine = both[:, :128], both[:, 128:]
        cos_ref[rows, :] = cosine
        sin_ref[rows, :] = sine
        x = x_ref[rows, :]
        for part, dst in enumerate((q_ref, k_ref, v_ref)):
            val = matmul(x, wqkv_ref[:, part * D : part * D + D], NN) + vec_ref[:, part * D : part * D + D]
            for g in range(3):
                cols = slice(g * 128, g * 128 + 128)
                piece = val[:, cols]
                if part < 2:
                    piece = turned(piece, cosine, sine, 1)
                dst[rows, cols] = piece.astype(jnp.bfloat16)
        return 0

    lax.fori_loop(0, count // tile, project, 0)

    def rest(t, _):
        rows = pl.ds(pl.multiple_of(t * tile, tile), tile)
        same = segc_ref[rows, :] == segr_ref[...]
        stats = jnp.zeros((tile, 128), jnp.float32)
        for g in range(3):
            cols = slice(g * 128, g * 128 + 128)
            q, k, v = q_ref[rows, cols], k_ref[:, cols], v_ref[:, cols]
            total = jnp.zeros((tile, 128), jnp.float32)
            for h in range(4):
                mine = jnp.where(head_mask(h, tile), q, jnp.zeros_like(q))
                scores = matmul(mine, k, NT) * SCALE
                scores = jnp.where(same, scores, -1e30)
                peak = jnp.max(scores, -1, keepdims=True)
                expo = jnp.exp(scores - peak)
                norm_sum = jnp.sum(expo, -1, keepdims=True)
                probs = (expo * (1.0 / norm_sum)).astype(jnp.bfloat16)
                part = matmul(probs, v, NN)
                total = jnp.where(head_mask(h, tile), part, total)
                stats = jnp.where(lanes((tile, 128)) == g * 4 + h, peak + jnp.log(norm_sum), stats)
            ctx_ref[rows, cols] = total.astype(jnp.bfloat16)
        resid = x_ref[rows, :].astype(jnp.float32) + (
            matmul(ctx_ref[rows, :], wout_ref[...], NN) + bias(vec_ref, 1, D)
        )
        normed, inv_one = norm(resid)
        n1_ref[rows, :] = normed
        hidden = normed * bias(vec_ref, 4, D) + bias(vec_ref, 5, D)
        low = hidden.astype(jnp.bfloat16)
        h1_ref[rows, :] = low
        mixed = jnp.zeros((tile, D), jnp.float32)
        for c in range(4):
            cols = slice(c * D, c * D + D)
            pre = matmul(low, wup_ref[:, cols], NN) + vec_ref[:, SPOTS[2] + c * D : SPOTS[2] + c * D + D]
            pre_ref[rows, cols] = pre
            act = gelu(pre).astype(jnp.bfloat16)
            act_ref[rows, cols] = act
            mixed = mixed + matmul(act, wdown_ref[cols, :], NN)
        normed, inv_two = norm(hidden + (mixed + bias(vec_ref, 3, D)))
        n2_ref[rows, :] = normed
        low = (normed * bias(vec_ref, 6, D) + bias(vec_ref, 7, D)).astype(jnp.bfloat16)
        h2_ref[rows, :] = low
        emitted = matmul(low, whead_ref[...], NT) + vec_ref[:, SPOTS[8] : SPOTS[8] + 96]
        inv_len = lax.rsqrt(jnp.sum(emitted * emitted, -1, keepdims=True) + 1e-06)
        out = emitted * inv_len
        out_ref[rows, :] = out
        low_ref[rows, :] = out.astype(jnp.bfloat16)
        place = lanes((tile, 128))
        stats = jnp.where(place == 12, inv_one, stats)
        stats = jnp.where(place == 13, inv_two, stats)
        stat_ref[rows, :] = jnp.where(place == 14, inv_len, stats)
        return 0

    lax.fori_loop(0, count // tile, rest, 0)


def encode_call(tokens, segment, table, weights, vectors, first, name):
    count = tokens.shape[0]
    f32, low = jnp.float32, jnp.bfloat16
    shapes = [
        (D, low), (D, low), (D, low), (D, low), (D, f32), (D, low), (FF, f32), (FF, low), (D, f32),
        (D, low), (96, f32), (96, low), (128, f32), (128, f32), (128, f32),
    ]
    outs = [jax.ShapeDtypeStruct((count, width), kind) for width, kind in shapes]
    if first:
        outs += [jax.ShapeDtypeStruct(w.shape, low) for w in weights]
    return pl.pallas_call(
        lambda *refs: encode_kernel(first, *refs), out_shape=outs, name=name
    )(tokens, segment[:, None], segment[None, :], table, *weights, vectors)


def backward_kernel(*refs):
    (
        grad_ref, segc_ref, segr_ref, q_ref, k_ref, v_ref, n1_ref, pre_ref, n2_ref, out_ref,
        stat_ref, cos_ref, sin_ref, wqkv_ref, wout_ref, wup_ref, wdown_ref, whead_ref, vec_ref,
    ) = refs[:19]
    yqkv_ref, yout_ref, yup_ref, ydown_ref, yhead_ref, packed_ref = refs[19:25]
    dk_ref, dv_ref, p_ref, s_ref, c_ref = refs[25:]
    count = q_ref.shape[0]
    tile = min(count, TILE)
    packed_ref[...] = jnp.zeros_like(packed_ref)
    dk_ref[...] = jnp.zeros_like(dk_ref)
    dv_ref[...] = jnp.zeros_like(dv_ref)

    def add(n, value, shift=0):
        at = SPOTS[n] + shift
        cols = slice(at, at + value.shape[1])
        packed_ref[:, cols] = packed_ref[:, cols] + jnp.sum(value, 0, keepdims=True)

    def norm_grad(grad, gain, normed, inv_std):
        scaled = grad * gain
        return inv_std * (
            scaled
            - jnp.mean(scaled, -1, keepdims=True)
            - normed * jnp.mean(scaled * normed, -1, keepdims=True)
        )

    def step(t, _):
        rows = pl.ds(pl.multiple_of(t * tile, tile), tile)
        stats = stat_ref[rows, :]
        grad_vec = grad_ref[rows, :] if len(grad_ref.shape) == 2 else jnp.sum(grad_ref[...], 0)
        output = out_ref[rows, :]
        emit = stats[:, 14:15] * (grad_vec - output * jnp.sum(grad_vec * output, -1, keepdims=True))
        add(8, emit)
        low = emit.astype(jnp.bfloat16)
        yhead_ref[rows, :] = low
        grad = matmul(low, whead_ref[...], NN)
        normed = n2_ref[rows, :]
        resid_two = norm_grad(grad, bias(vec_ref, 6, D), normed, stats[:, 13:14])
        add(6, grad * normed)
        add(7, grad)
        add(3, resid_two)
        low = resid_two.astype(jnp.bfloat16)
        ydown_ref[rows, :] = low
        grad = resid_two
        for c in range(4):
            cols = slice(c * D, c * D + D)
            pre = matmul(low, wdown_ref[cols, :], NT) * gelu_slope(pre_ref[rows, cols])
            add(2, pre, c * D)
            pre = pre.astype(jnp.bfloat16)
            yup_ref[rows, cols] = pre
            grad = grad + matmul(pre, wup_ref[:, cols], NT)
        normed = n1_ref[rows, :]
        resid_one = norm_grad(grad, bias(vec_ref, 4, D), normed, stats[:, 12:13])
        add(4, grad * normed)
        add(5, grad)
        add(1, resid_one)
        low = resid_one.astype(jnp.bfloat16)
        yout_ref[rows, :] = low
        grad_ctx = matmul(low, wout_ref[...], NT).astype(jnp.bfloat16)
        same = segc_ref[rows, :] == segr_ref[...]
        cosine, sine = cos_ref[rows, :], sin_ref[rows, :]
        for g in range(3):
            cols = slice(g * 128, g * 128 + 128)
            q, k, v = q_ref[rows, cols], k_ref[:, cols], v_ref[:, cols]
            dctx = grad_ctx[:, cols]
            dq = jnp.zeros((tile, 128), jnp.float32)
            for h in range(4):
                mask = head_mask(h, tile)
                mine = jnp.where(mask, q, jnp.zeros_like(q))
                back = jnp.where(mask, dctx, jnp.zeros_like(dctx))
                place = slice(h * tile, h * tile + tile)
                scores = matmul(mine, k, NT) * SCALE
                head = g * 4 + h
                probs = jnp.where(same, jnp.exp(scores - stats[:, head : head + 1]), 0.0)
                gprob = matmul(back, v, NT)
                weighed = gprob * probs
                gscore = weighed - probs * jnp.sum(weighed, -1, keepdims=True)
                gscore = gscore.astype(jnp.bfloat16)
                p_ref[place, :] = probs.astype(jnp.bfloat16)
                s_ref[place, :] = gscore
                c_ref[place, :] = back
                c_ref[4 * tile + h * tile : 4 * tile + h * tile + tile, :] = mine
                dq = jnp.where(mask, matmul(gscore, k, NN), dq)
            dv_ref[:, cols] = dv_ref[:, cols] + matmul(p_ref[...], c_ref[: 4 * tile, :], TN)
            dk_ref[:, cols] = dk_ref[:, cols] + matmul(s_ref[...], c_ref[4 * tile :, :], TN)
            dq = turned(dq * SCALE, cosine, sine, -1)
            add(0, dq, g * 128)
            yqkv_ref[rows, cols] = dq.astype(jnp.bfloat16)
        return 0

    lax.fori_loop(0, count // tile, step, 0)

    def last(t, _):
        rows = pl.ds(pl.multiple_of(t * tile, tile), tile)
        cosine, sine = cos_ref[rows, :], sin_ref[rows, :]
        for g in range(3):
            cols = slice(g * 128, g * 128 + 128)
            dk = turned(dk_ref[rows, cols] * SCALE, cosine, sine, -1)
            dv = dv_ref[rows, cols]
            add(0, dk, D + g * 128)
            add(0, dv, 2 * D + g * 128)
            yqkv_ref[rows, D + g * 128 : D + g * 128 + 128] = dk.astype(jnp.bfloat16)
            yqkv_ref[rows, 2 * D + g * 128 : 2 * D + g * 128 + 128] = dv.astype(jnp.bfloat16)
        return 0

    lax.fori_loop(0, count // tile, last, 0)


def backward_call(grad, segment, kept, weights, vectors, name):
    q, k, v, _, n1, _, pre, _, n2, _, out, _, stat, cosine, sine = kept
    count = q.shape[0]
    tile = min(count, TILE)
    f32, low = jnp.float32, jnp.bfloat16
    outs = [jax.ShapeDtypeStruct((count, width), low) for width in (3 * D, D, FF, D, 96)]
    return pl.pallas_call(
        backward_kernel,
        out_shape=outs + [jax.ShapeDtypeStruct((1, 5120), f32)],
        scratch_shapes=[
            pltpu.VMEM((count, D), f32),
            pltpu.VMEM((count, D), f32),
            pltpu.VMEM((4 * tile, count), low),
            pltpu.VMEM((4 * tile, count), low),
            pltpu.VMEM((8 * tile, 128), low),
        ],
        name=name,
    )(
        grad, segment[:, None], segment[None, :], q, k, v, n1, pre, n2, out, stat, cosine, sine,
        *weights, vectors,
    )


def early_kernel(me_ref, *refs):
    fac_refs, err_refs, early_ref, parts_ref = refs[:5], refs[5:10], refs[10], refs[11]
    at = to = 0
    for n, (fac_ref, err_ref) in enumerate(zip(fac_refs, err_refs)):
        wide = fac_ref.shape[1]
        head = n == 4
        quarter = (err_ref.shape[1] if head else 4 * err_ref.shape[0]) // 4
        parts = jnp.concatenate(split_rows(fac_ref[...]), 0)
        parts_ref[:, to : to + wide] = parts
        to += wide
        total = jnp.zeros((24, quarter), jnp.float32)
        if head:
            total = jnp.zeros((24, 4 * quarter), jnp.float32)
        for part in split_rows(err_ref[...]):
            total = total + matmul(parts, part, NN if head else NT)
        total = total[:8] + total[8:16] + total[16:24]
        spread_out = total if head else jnp.concatenate([total] * 4, 1)
        spot = lanes(spread_out.shape) // quarter
        early_ref[:, at : at + 4 * quarter] = jnp.where(spot == me_ref[0], spread_out, 0.0)
        at += 4 * quarter


def grads_kernel(me_ref, *refs):
    acts, parts_ref, early_ref, packed_refs = refs[:20], refs[20], refs[21], refs[22:24]
    a_ref, b_ref, left_ref = refs[24:]
    me = me_ref[0]

    def turns(quarter):
        turn = quarter ^ me
        return (turn & 1) * 2 + (turn >> 1), turn

    def place(block, value):
        low = value.astype(jnp.bfloat16)
        for quarter in range(4):
            a_at, b_at = turns(quarter)
            rows = low[quarter * 96 : quarter * 96 + 96]
            if block < 6:
                a_ref[a_at, block * 96 : block * 96 + 96, :] = rows
            elif block < 12:
                b_ref[b_at, (block - 6) * 96 : (block - 6) * 96 + 96, :] = rows
            else:
                b_ref[b_at, 576:600, :] = low[quarter * 24 : quarter * 24 + 24]
                b_ref[b_at, 600:608, :] = jnp.zeros((8, 384), jnp.bfloat16)

    block = at = to = 0
    for n in range(5):
        dx_ref, qx_ref, dy_ref, qy_ref = acts[4 * n : 4 * n + 4]
        parts = parts_ref[:, to : to + dy_ref.shape[1]]
        to += dy_ref.shape[1]
        tall_d = matmul(dy_ref[...], parts, NT)
        tall_q = matmul(qy_ref[...], parts, NT)
        parts = []
        for tall in (tall_d, tall_q):
            tall = tall[:, :8] + tall[:, 8:16] + tall[:, 16:24]
            parts.append(jnp.concatenate(split_rows(tall), 1))
        wide = dx_ref.shape[1]
        left = matmul(parts[0], dx_ref[...], TN) + matmul(parts[1], qx_ref[...], TN)
        left_ref[:, at : at + wide] = (
            left[:8] + left[8:16] + left[16:24] + early_ref[:, at : at + wide]
        )
        at += wide
        if n == 4:
            place(
                block,
                matmul(dy_ref[...], dx_ref[...], TN) + matmul(qy_ref[...], qx_ref[...], TN),
            )
            continue
        for k in range(wide // 384):
            rows = slice(k * 384, k * 384 + 384)
            dxt, qxt = dx_ref[:, rows].T, qx_ref[:, rows].T
            for c in range(dy_ref.shape[1] // 384):
                cols = slice(c * 384, c * 384 + 384)
                place(block, matmul(dxt, dy_ref[:, cols], NN) + matmul(qxt, qy_ref[:, cols], NN))
                block += 1
    side = packed_refs[0].shape[1] // 8
    for r in range(8):
        cols = slice(r * side, r * side + side)
        left_ref[r : r + 1, at : at + side] = packed_refs[0][:, cols] + packed_refs[1][:, cols]
    left_ref[:, at + side :] = jnp.zeros((8, left_ref.shape[1] - at - side), jnp.float32)


def factors_kernel(bounds, me_ref, left_ref, *refs):
    acts, err_refs = refs[:20], refs[20:25]
    basis_ref, right_ref = refs[25:]
    me = me_ref[0]
    basis_kernel(bounds, left_ref, basis_ref)
    at = 0
    for n, (lo, hi) in enumerate(bounds):
        dx_ref, qx_ref, dy_ref, qy_ref = acts[4 * n : 4 * n + 4]
        base = basis_ref[:, lo:hi]
        base_parts = jnp.concatenate(split_rows(base), 0)
        total = None
        for x_ref, y_ref in ((dx_ref, dy_ref), (qx_ref, qy_ref)):
            tall = matmul(x_ref[...], base_parts, NT)
            tall = tall[:, :8] + tall[:, 8:16] + tall[:, 16:24]
            right = matmul(jnp.concatenate(split_rows(tall), 1), y_ref[...], TN)
            total = right if total is None else total + right
        quarter = (hi - lo) // 4
        if n == 4:
            share = jnp.where(lanes(base.shape) // quarter == me, base, 0.0)
        else:
            share = jnp.zeros((8, quarter), jnp.float32)
            for k in range(4):
                share = jnp.where(me == k, base[:, k * quarter : (k + 1) * quarter], share)
        share = jnp.concatenate(split_rows(share), 0)
        for part in split_rows(err_refs[n][...]):
            total = total + matmul(share, part, NT if n == 4 else NN)
        wide = dy_ref.shape[1]
        right_ref[:, at : at + wide] = total[:8] + total[8:16] + total[16:24]
        at += wide
    right_ref[:, at:] = jnp.zeros((8, right_ref.shape[1] - at), jnp.float32)


HEIGHTS = (D, D, D, FF, D)


def weight_kernel(spans, rate, *refs):
    right_ref, summed_ref, vec_ref, vec_mom_ref = refs[:4]
    ins, outs = refs[4:19], refs[19:]
    for n, (at, span) in enumerate(spans):
        basis_ref, mom_ref, w_ref = ins[3 * n : 3 * n + 3]
        new_w_ref, new_m_ref = outs[2 * n : 2 * n + 2]

        def update(approx):
            moved = MOMENTUM * mom_ref[...] + approx
            new_m_ref[...] = moved
            new_w_ref[...] = w_ref[...] - rate * moved

        right = right_ref[:, at : at + span]
        if n < 4:
            update(matmul(basis_ref[...], right, NN))
        else:
            pl.when(pl.program_id(0) == 0)(
                lambda: update(lax.dot_general(
                    right, basis_ref[...], (((0,), (1,)), ((), ())),
                    preferred_element_type=jnp.float32,
                ))
            )

    @pl.when(pl.program_id(0) == 0)
    def _():
        first = sum(HEIGHTS)
        side = 640
        for r in range(8):
            width = min(side, vec_ref.shape[1] - r * side)
            cols = slice(r * side, r * side + width)
            moved = (
                MOMENTUM * vec_mom_ref[:, cols] + summed_ref[r : r + 1, first : first + width]
            )
            outs[11][:, cols] = moved
            outs[10][:, cols] = vec_ref[:, cols] - rate * moved


def error_kernel(spans, replicas, me_ref, right_ref, *refs):
    a_refs, b_refs = refs[:2], refs[2:4]
    basis_refs, err_refs, new_refs = refs[4:9], refs[9:14], refs[14:]
    share = 1.0 / replicas
    quarter = pl.program_id(0)
    turn = quarter ^ me_ref[0]

    def pick(pair, near, rows):
        return jnp.where(near, pair[0][0, rows, :], pair[1][0, rows, :]).astype(jnp.float32)

    def grad(block):
        if block < 6:
            return pick(a_refs, (turn & 1) == 0, slice(block * 96, block * 96 + 96))
        return pick(b_refs, (turn >> 1) == 0, slice((block - 6) * 96, (block - 6) * 96 + 96))

    block = 0
    for n, (at, span) in enumerate(spans):
        right = right_ref[:, at : at + span]
        if n == 3:
            for k in range(4):
                approx = matmul(basis_refs[n][k], right, NN)
                new_refs[n][k] = grad(block) + err_refs[n][k] - approx * share
                block += 1
        elif n == 4:
            approx = lax.dot_general(
                right, basis_refs[n][...], (((0,), (1,)), ((), ())),
                preferred_element_type=jnp.float32,
            )
            base = err_refs[n][...] - approx * share
            near = (turn >> 1) == 0
            rows = pl.ds(pl.multiple_of(quarter * 24, 8), 24)
            new_refs[n][...] = jnp.where(quarter == 0, base, new_refs[n][...])
            new_refs[n][rows, :] = new_refs[n][rows, :] + pick(b_refs, near, slice(576, 600))
        else:
            approx = matmul(basis_refs[n][...], right, NN)
            for c in range(span // 384):
                cols = slice(c * 384, c * 384 + 384)
                new_refs[n][:, cols] = grad(block) + err_refs[n][:, cols] - approx[:, cols] * share
                block += 1


def whole(value):
    return pl.BlockSpec(value.shape, lambda i, me: (0,) * value.ndim)


def exchange(value, turn):
    return lax.ppermute(value, "stream", [(i, i ^ turn) for i in range(4)])


def stream_sum(a, b):
    def add(first, second):
        return (first.astype(jnp.float32) + second.astype(jnp.float32)).astype(jnp.bfloat16)

    both = []
    got = [exchange(a[2:], 1), exchange(b[2:], 2)]
    half = [add(a[:2], got[0]), add(b[:2], got[1])]
    got = [exchange(half[0][1], 2), exchange(half[1][1], 1)]
    full = [add(half[0][0], got[0]), add(half[1][0], got[1])]
    got = [exchange(full[0], 2), exchange(full[1], 1)]
    pair = [jnp.stack([one, two], 0) for one, two in zip(full, got)]
    last = [exchange(pair[0], 1), exchange(pair[1], 2)]
    return pair[0], last[0], pair[1], last[1]


def shards(
    query_embeds,
    doc_embeds,
    doc_segments,
    candidates,
    neg_counts,
    w_qkv,
    w_out,
    w_up,
    w_down,
    w_head,
    vectors,
    mom_qkv,
    mom_out,
    mom_up,
    mom_down,
    mom_head,
    mom_vectors,
    err_qkv,
    err_out,
    err_up,
    err_down,
    err_head,
    fac_qkv,
    fac_out,
    fac_up,
    fac_down,
    fac_head,
):
    streams, replicas = lax.axis_size("stream"), lax.axis_size("replica")
    devices = streams * replicas
    my_stream, me = lax.axis_index("stream"), lax.axis_index(AXES)
    qdev, qlen, width = query_embeds.shape
    row = doc_embeds.shape[1]
    qtok = qdev * qlen
    weights = (w_qkv, w_out, w_up, w_down, w_head.T)
    moms = (mom_qkv, mom_out, mom_up, mom_down, mom_head.T)
    errs = (err_qkv[0], err_out[0], err_up[0], err_down[0], err_head[0].T)
    fac_rows = [fac.T for fac in (fac_qkv, fac_out, fac_up, fac_down, fac_head)]
    sizes = [v.shape for v in (w_qkv, w_out, w_up, w_down, w_head)]
    vec_row = vectors[None, :]
    table = jnp.asarray(turn_table())
    query_in = query_embeds.reshape(qtok, width)
    query_seg = jnp.arange(qtok, dtype=jnp.int32) // qlen
    *query_kept, m0, m1, m2, m3, m4 = encode_call(
        query_in, query_seg, table, weights, vec_row,
        True, "encode_queries",
    )
    mats = (m0, m1, m2, m3, m4)
    all_query = spread(query_kept[11], devices)

    doc_in = doc_embeds[0]
    doc_seg = doc_segments[0]
    doc_kept = encode_call(
        doc_in, doc_seg, table, mats, vec_row, False, "encode_documents"
    )
    doc_low = doc_kept[11]
    pdim = doc_low.shape[1]

    tokens = devices * qtok
    rows_all = all_query.reshape(tokens, pdim)
    segment = doc_segments[0]
    sims = (
        lax.dot_general(
            doc_low, rows_all, (((1,), (1,)), ((), ())), preferred_element_type=jnp.float32
        )
        / SOFT
    )
    weight = jnp.exp(sims)
    segmask = (segment[None, :] == jnp.arange(NSEG)[:, None]).astype(jnp.float32)
    totals = jnp.stack(
        [jnp.sum(jnp.where((segment == d)[:, None], weight, 0.0), 0) for d in range(NSEG)], 0
    )
    scores = (SOFT * jnp.log(totals)).reshape(NSEG, devices, qdev, qlen).sum(-1)
    scores = scores.reshape(NSEG, devices * qdev)
    table = spread(scores, devices).reshape(devices * NSEG, devices * qdev)
    me_stream = my_stream[None].astype(jnp.int32)
    height, wide = sum(m for m, _ in sizes), sum(n for _, n in sizes)
    early, fac_parts = pl.pallas_call(
        early_kernel,
        grid_spec=pltpu.PrefetchScalarGridSpec(
            num_scalar_prefetch=1,
            grid=(1,),
            in_specs=[whole(v) for v in fac_rows]
            + [
                pl.BlockSpec((e.shape[0] // 4, e.shape[1]), lambda i, me: (me[0], 0))
                for e in errs[:4]
            ]
            + [whole(errs[4])],
            out_specs=[
                pl.BlockSpec((8, height), lambda i, me: (0, 0)),
                pl.BlockSpec((24, wide), lambda i, me: (0, 0)),
            ],
        ),
        out_shape=[
            jax.ShapeDtypeStruct((8, height), jnp.float32),
            jax.ShapeDtypeStruct((24, wide), jnp.bfloat16),
        ],
        name="early",
    )(me_stream, *fac_rows, *lax.optimization_barrier((errs, scores))[0])
    docs = jnp.arange(devices * NSEG)
    slots = jnp.arange(candidates.shape[1])
    named = (candidates[None] == docs[:, None, None]) & (slots <= neg_counts[:, None])[None]
    first = (candidates[:, 0][None] == docs[:, None]).astype(jnp.float32)
    listed = jnp.any(named, -1)
    logits = jnp.where(listed, table, -1e30)
    peak = jnp.max(logits, 0, keepdims=True)
    expo = jnp.exp(logits - peak)
    total = jnp.sum(expo, 0, keepdims=True)
    total_queries = candidates.shape[0]
    losses = peak[0] + jnp.log(total[0]) - jnp.sum(table * first, 0)
    loss = jnp.mean(losses)
    grad_table = (expo / total - first) / total_queries
    own = lax.dynamic_slice_in_dim(grad_table, me * NSEG, NSEG, 0)
    per_token = jnp.repeat(own, qlen, axis=1) / totals
    spots = jnp.sum(segmask[:, :, None] * per_token[:, None, :], 0)
    sim_low = (weight * spots).astype(jnp.bfloat16)
    query_grad = lax.dot_general(
        sim_low, doc_low, (((0,), (0,)), ((), ())), preferred_element_type=jnp.float32
    ).reshape(devices, qtok, pdim)
    query_local = lax.all_to_all(query_grad, AXES, 0, 0, tiled=True)
    doc_grad = jnp.dot(sim_low, rows_all, preferred_element_type=jnp.float32)

    *doc_out, doc_packed = backward_call(
        doc_grad, doc_seg, doc_kept, mats, vec_row, "backward_documents"
    )
    *query_out, query_packed = backward_call(
        query_local, query_seg, query_kept, mats, vec_row, "backward_queries"
    )
    inputs = ((doc_in, query_in),) + tuple((doc_kept[n], query_kept[n]) for n in (3, 5, 7, 9))
    acts = [
        v for (dx, qx), dy, qy in zip(inputs, doc_out, query_out) for v in (dx, qx, dy, qy)
    ]
    edges = [0]
    for m, _ in sizes:
        edges.append(edges[-1] + m)
    bounds = list(zip(edges[:-1], edges[1:]))
    side = doc_packed.shape[1] // 8
    full = edges[-1] + side
    full += -full % (128 * devices) if devices <= 32 else -full % (16 * devices)
    a_grads, b_grads, left = pl.pallas_call(
        grads_kernel,
        grid_spec=pltpu.PrefetchScalarGridSpec(
            num_scalar_prefetch=1,
            grid=(1,),
            in_specs=[whole(v) for v in acts + [fac_parts, early, doc_packed, query_packed]],
            out_specs=[
                pl.BlockSpec((4, 576, D), lambda i, me: (0, 0, 0)),
                pl.BlockSpec((4, 608, D), lambda i, me: (0, 0, 0)),
                pl.BlockSpec((8, full), lambda i, me: (0, 0)),
            ],
        ),
        out_shape=[
            jax.ShapeDtypeStruct((4, 576, D), jnp.bfloat16),
            jax.ShapeDtypeStruct((4, 608, D), jnp.bfloat16),
            jax.ShapeDtypeStruct((8, full), jnp.float32),
        ],
        name="grads",
    )(me_stream, *acts, fac_parts, early, doc_packed, query_packed)
    sums = stream_sum(a_grads, b_grads)

    summed = all_sum(left)

    wide += -wide % (128 * devices) if devices <= 32 else -wide % (128 * devices // 8)
    basis, right = pl.pallas_call(
        lambda *refs: factors_kernel(bounds, *refs),
        grid_spec=pltpu.PrefetchScalarGridSpec(
            num_scalar_prefetch=1,
            grid=(1,),
            in_specs=[whole(summed)]
            + [whole(v) for v in acts]
            + [
                pl.BlockSpec((e.shape[0] // 4, e.shape[1]), lambda i, me: (me[0], 0))
                for e in errs[:4]
            ]
            + [whole(errs[4])],
            out_specs=[
                pl.BlockSpec((8, edges[-1]), lambda i, me: (0, 0)),
                pl.BlockSpec((8, wide), lambda i, me: (0, 0)),
            ],
        ),
        out_shape=[
            jax.ShapeDtypeStruct((8, edges[-1]), jnp.float32),
            jax.ShapeDtypeStruct((8, wide), jnp.float32),
        ],
        name="factors",
    )(me_stream, summed, *acts, *errs)
    joined = all_sum(right)
    rights, spans, at = [], [], 0
    for _, n in sizes:
        rights.append(joined[:, at : at + n])
        spans.append((at, n))
        at += n

    rate = RATE * qdev * math.sqrt(devices / (row + qtok))
    firsts, seconds = thirds(basis), thirds(joined)
    left_parts = jnp.concatenate([firsts[k] for k in (0, 0, 1, 0, 1, 2)], 0).T
    right_parts = jnp.concatenate([seconds[k] for k in (0, 1, 0, 2, 1, 0)], 0)
    left_parts = [left_parts[lo:hi] for lo, hi in bounds]
    steps = 6

    def part_spec(value, head):
        if head:
            return pl.BlockSpec(value.shape, lambda i: (0, 0))
        return pl.BlockSpec((value.shape[0] // steps, value.shape[1]), lambda i: (i, 0))

    trios = list(zip(left_parts, moms, weights))
    moved = pl.pallas_call(
        lambda *refs: weight_kernel(spans, rate, *refs),
        grid=(steps,),
        in_specs=[part_spec(v, True) for v in (right_parts, summed, vec_row, vec_row)]
        + [part_spec(v, n == 4) for n, trio in enumerate(trios) for v in trio],
        out_specs=[part_spec(w, n == 4) for n, w in enumerate(weights) for _ in range(2)]
        + [part_spec(vec_row, True)] * 2,
        out_shape=[jax.ShapeDtypeStruct(w.shape, jnp.float32) for w in weights for _ in range(2)]
        + [jax.ShapeDtypeStruct(vec_row.shape, jnp.float32)] * 2,
        name="weights",
    )(right_parts, summed, vec_row, mom_vectors[None, :], *[v for trio in trios for v in trio])
    new_w, new_m = list(moved[0:10:2]), list(moved[1:10:2])
    new_w[4], new_m[4] = new_w[4].T, new_m[4].T
    new_vec, vec_mom = moved[10][0], moved[11][0]

    def quartered(value):
        if value.shape[0] == 4 * D:
            return value.reshape(4, D, value.shape[1])
        return value

    def quarter_spec(value):
        if len(value.shape) == 3:
            return pl.BlockSpec((4, D // 4, value.shape[2]), lambda q, me: (0, q, 0))
        if value.shape[0] != D or value is left_parts[4]:
            return pl.BlockSpec(value.shape, lambda q, me: (0, 0))
        return pl.BlockSpec((D // 4, value.shape[1]), lambda q, me: (q, 0))

    rows = [quartered(v) for v in left_parts] + [quartered(v) for v in errs]
    out = [jax.ShapeDtypeStruct(quartered(e).shape, jnp.float32) for e in errs]
    new_e = pl.pallas_call(
        lambda *refs: error_kernel(spans, replicas, *refs),
        grid_spec=pltpu.PrefetchScalarGridSpec(
            num_scalar_prefetch=1,
            grid=(4,),
            in_specs=[
                pl.BlockSpec(right_parts.shape, lambda q, me: (0, 0)),
                pl.BlockSpec((1, 576, D), lambda q, me: ((q ^ me[0]) >> 1, 0, 0)),
                pl.BlockSpec((1, 576, D), lambda q, me: ((q ^ me[0]) >> 1, 0, 0)),
                pl.BlockSpec((1, 608, D), lambda q, me: ((q ^ me[0]) & 1, 0, 0)),
                pl.BlockSpec((1, 608, D), lambda q, me: ((q ^ me[0]) & 1, 0, 0)),
            ]
            + [quarter_spec(v) for v in rows],
            out_specs=[quarter_spec(v) for v in out],
        ),
        out_shape=out,
        name="errors",
    )(me_stream, right_parts, *sums, *rows)
    new_e = [v.reshape((1,) + e.shape) for v, e in zip(new_e, errs)]
    new_e[4] = jnp.swapaxes(new_e[4], 1, 2)
    return (
        loss,
        *new_w,
        new_vec,
        *new_m,
        vec_mom,
        *new_e,
        *[right.T for right in rights],
    )


def solution(mesh):
    return jax.shard_map(
        shards,
        mesh=mesh,
        in_specs=(
            P(("stream", "replica"), None, None),
            P(("stream", "replica"), None, None),
            P(("stream", "replica"), None),
            P(),
            P(),
            P(),
            P(),
            P(),
            P(),
            P(),
            P(),
            P(),
            P(),
            P(),
            P(),
            P(),
            P(),
            P("replica", None, None),
            P("replica", None, None),
            P("replica", None, None),
            P("replica", None, None),
            P("replica", None, None),
            P(),
            P(),
            P(),
            P(),
            P(),
        ),
        out_specs=(
            P(),
            P(),
            P(),
            P(),
            P(),
            P(),
            P(),
            P(),
            P(),
            P(),
            P(),
            P(),
            P(),
            P("replica", None, None),
            P("replica", None, None),
            P("replica", None, None),
            P("replica", None, None),
            P("replica", None, None),
            P(),
            P(),
            P(),
            P(),
            P(),
        ),
        check_vma=False,
    )
```

profile of v0, /device:TPU:0, one launch (start us, length us, event | category | flops | bytes accessed | tf_op | source)
XLA Modules:
  0.0 246.0 jit_solution(3215955459081480151)
XLA Ops:
  1.8 9.8 %encode_queries.1 = (bf16[64,384]{1,0:T(8,128)(2,1)}, bf16[64,384]{1,0:T(8,128)(2,1)}, bf16[64,384]{1,0:T(8,128)(2,1)}, bf16[64,384]{1,0:T(8,128)(2,1)}, f32[64,...) custom-call(bf16[64,384]{1,0:T(8,128)(2,1)} %bitcast.141, ...), custom_call_target="tpu_custom_call" | custom-call | tf_op jit(solution)/shard_map/encode_queries/pallas_call | solution.py:435
  11.6 1.6 broadcast_in_dim.94
  13.3 7.5 %all-to-all-start = ((bf16[32,64,96]{2,1,0:T(8,128)(2,1)}), bf16[32,64,96]{2,1,0:T(8,128)(2,1)S(1)}, u32[]{:S(2)}, u32[]{:S(2)}) async-start(bf16[32,64,96]{2,1,0:T(8,128)(2,1)} %broadcast_in_dim.94), calls=%async_computation | async-start | bytes 1048576 | tf_op jit(solution)/shard_map/all_to_all | solution.py:233
  22.3 16.5 %encode_documents.1 = (bf16[512,384]{1,0:T(8,128)(2,1)}, bf16[512,384]{1,0:T(8,128)(2,1)}, bf16[512,384]{1,0:T(8,128)(2,1)}, bf16[512,384]{1,0:T(8,128)(2,1)}, f...) custom-call(bf16[512,384]{1,0:T(8,128)(2,1)} %bitcast.119, ...), custom_call_target="tpu_custom_call" | custom-call | tf_op jit(solution)/shard_map/encode_documents/pallas_call | solution.py:435
  38.9 5.5 %select_reduce_fusion.3 = (f32[2048]{0:T(1024)S(1)}, f32[2048]{0:T(1024)S(1)}, f32[2048]{0:T(1024)S(1)}, f32[2048]{0:T(1024)S(1)}, f32[512,2048]{1,0:T(8,128)}) fusion(pred[512]{0:T(512)(128)(4,1)S(1)} %get-tuple-element.190, pred[512]{0:T(512)(128)(4,1)S(1)} %get-tuple-element.188, pred[512]{0:T(512)(128)(4,1)S(1)} %get-tuple-element.189, ...), kind=kOutput, calls=%fused_computation.5 | convolution fusion | flops 210755584 | bytes 4720640 | tf_op jit(solution)/shard_map/dot_general | solution.py:851
  45.8 5.8 %all-to-all-start.1 = ((f32[32,1,256]{2,1,0:T(1,128)}), f32[32,1,256]{2,1,0:T(1,128)S(1)}, u32[]{:S(2)}, u32[]{:S(2)}) async-start(f32[32,1,256]{2,1,0:T(1,128)} %reshape.315), calls=%async_computation.1 | async-start | bytes 65536 | tf_op jit(solution)/shard_map/all_to_all | solution.py:233
  51.7 7.2 %all-to-all-done.1 = f32[32,1,256]{2,1,0:T(1,128)S(1)} async-done(((f32[32,1,256]{2,1,0:T(1,128)}), f32[32,1,256]{2,1,0:T(1,128)S(1)}, u32[]{:S(2)}, u32[]{:S(2)}) %all-to-all-start.1) | async-done | bytes 32800 | tf_op jit(solution)/shard_map/all_to_all | solution.py:233
  61.0 1.2 multiply_reduce_fusion
  63.2 1.0 multiply_convert_fusion
  64.2 1.7 fusion.17
  65.9 2.6 %all-to-all-start.2 = ((f32[32,64,96]{2,1,0:T(8,128)}), f32[32,64,96]{2,1,0:T(8,128)S(1)}, u32[]{:S(2)}, u32[]{:S(2)}) async-start(f32[32,64,96]{2,1,0:T(8,128)} %bitcast.16), calls=%async_computation.2 | async-start | bytes 2097152 | tf_op jit(solution)/shard_map/all_to_all | solution.py:908
  68.6 3.1 %early.1 = (f32[8,3072]{1,0:T(8,128)}, bf16[24,3552]{1,0:T(8,128)(2,1)}) custom-call(s32[1]{0:T(128)} %bitcast.10.me_ref.refs_0_, f32[8,1152]{1,0:T(8,128)} %bitcast.154, f32[8,384]{1,0:T(8,128)} %bitcast.160, f32[8,1536]{1,0:T(8,128)} %bitcast.153, f32[8,384]{1,0:T(8,128)} %bitcast.161, f32[8,96]{1,0:T(8,128)} %bitcast.162, f32[384,1152]{1,0:T(8,128)} %bitcast.108, ...), custom_call_target="tpu_custom_call" | custom-call | tf_op jit(solution)/shard_map/early/pallas_call | solution.py:866
  71.7 2.4 fusion.16.refs_0_
  74.1 23.3 %backward_documents.1 = (bf16[512,1152]{1,0:T(8,128)(2,1)}, bf16[512,384]{1,0:T(8,128)(2,1)}, bf16[512,1536]{1,0:T(8,128)(2,1)}, bf16[512,384]{1,0:T(8,128)(2,1)...) custom-call(f32[512,96]{1,0:T(8,128)} %fusion.16.refs_0_, s32[512,1]{1,0:T(8,128)} %copy.93.refs_1_, s32[1,512]{1,0:T(1,128)} %refs_2_.3, ...), custom_call_target="tpu_custom_call" | custom-call | tf_op jit(solution)/shard_map/backward_documents/pallas_call | solution.py:554
  97.5 1.0 copy-done
  98.4 8.0 %backward_queries.1 = (bf16[64,1152]{1,0:T(8,128)(2,1)}, bf16[64,384]{1,0:T(8,128)(2,1)}, bf16[64,1536]{1,0:T(8,128)(2,1)}, bf16[64,384]{1,0:T(8,128)(2,1)}, bf16[64,96]{1,0:T(8,128)(2,1)}, /*index=5*/f32[1,5120]{1,0:T(1,128)}) custom-call(f32[32,64,96]{2,1,0:T(8,128)} %copy-done, s32[64,1]{1,0:T(8,128)} %add_select_fusion.refs_1_, ...), custom_call_target="tpu_custom_call" | custom-call | tf_op jit(solution)/shard_map/backward_queries/pallas_call | solution.py:554
  106.5 13.0 %grads.1 = (bf16[4,576,384]{2,1,0:T(8,128)(2,1)}, bf16[4,608,384]{2,1,0:T(8,128)(2,1)}, f32[8,4096]{1,0:T(8,128)}) custom-call(s32[1]{0:T(128)} %bitcast.10.me_ref.refs_0_, bf16[512,384]{1,0:T(8,128)(2,1)} %bitcast.120, bf16[64,384]{1,0:T(8,128)(2,1)} %bitcast.142, bf16[512,1152]{1,0:T(8,128)(2,1)} %get-tuple-element.116.refs_2_.refs_4_, ...), custom_call_target="tpu_custom_call" | custom-call | tf_op jit(solution)/shard_map/grads/pallas_call | solution.py:928
  119.5 14.0 %all_to_all.35 = f32[32,8,128]{2,1,0:T(8,128)S(1)} all-to-all(f32[32,8,128]{2,1,0:T(8,128)} %bitcast.148), channel_id=1, replica_groups=mesh['stream'=4,'replica'=8] {'stream','replica'}, dimensions={0} | all-to-all | bytes 262144 | tf_op jit(solution)/shard_map/all_to_all | solution.py:240
  134.2 2.6 %all-to-all-start.4 = ((f32[32,8,128]{2,1,0:T(8,128)}), f32[32,8,128]{2,1,0:T(8,128)S(1)}, u32[]{:S(2)}, u32[]{:S(2)}) async-start(f32[32,8,128]{2,1,0:T(8,128)} %broadcast_in_dim.105), calls=%async_computation.4 | async-start | bytes 262144 | tf_op jit(solution)/shard_map/all_to_all | solution.py:233
  138.0 2.2 slice.68
  140.2 1.7 collective-permute-start.4
  141.9 1.0 slice.64
  142.9 1.5 collective-permute-start
  145.7 11.1 %factors.1 = (f32[8,3072]{1,0:T(8,128)}, f32[8,4096]{1,0:T(8,128)}) custom-call(s32[1]{0:T(128)} %bitcast.10.me_ref.refs_0_, f32[8,4096]{1,0:T(8,128)} %bitcast.131, bf16[512,384]{1,0:T(8,128)(2,1)} %bitcast.121, bf16[64,384]{1,0:T(8,128)(2,1)} %bitcast.143, bf16[512,1152]{1,0:T(8,128)(2,1)} %get-tuple-element.116.refs_2_.refs_4_, ...), custom_call_target="tpu_custom_call" | custom-call | tf_op jit(solution)/shard_map/factors/pallas_call | solution.py:952
  156.8 0.9 constant_dynamic-update-slice_fusion.9
  157.7 0.9 constant_dynamic-update-slice_fusion.8
  158.6 0.9 constant_dynamic-update-slice_fusion.7
  159.5 0.9 constant_dynamic-update-slice_fusion.6
  160.4 0.9 constant_dynamic-update-slice_fusion.5
  161.3 3.2 %all-to-all-start.5 = ((f32[32,8,128]{2,1,0:T(8,128)}), f32[32,8,128]{2,1,0:T(8,128)S(1)}, u32[]{:S(2)}, u32[]{:S(2)}) async-start(f32[32,8,128]{2,1,0:T(8,128)} %bitcast.147), calls=%async_computation.5 | async-start | bytes 262144 | tf_op jit(solution)/shard_map/all_to_all | solution.py:240
  164.5 0.9 fusion.9
  167.4 5.3 %all-to-all-done.5 = f32[32,8,128]{2,1,0:T(8,128)S(1)} async-done(((f32[32,8,128]{2,1,0:T(8,128)}), f32[32,8,128]{2,1,0:T(8,128)S(1)}, u32[]{:S(2)}, u32[]{:S(2)}) %all-to-all-start.5) | async-done | bytes 131104 | tf_op jit(solution)/shard_map/all_to_all | solution.py:240
  173.4 2.6 %all-to-all-start.6 = ((f32[32,8,128]{2,1,0:T(8,128)}), f32[32,8,128]{2,1,0:T(8,128)S(1)}, u32[]{:S(2)}, u32[]{:S(2)}) async-start(f32[32,8,128]{2,1,0:T(8,128)} %broadcast_in_dim.106), calls=%async_computation.6 | async-start | bytes 262144 | tf_op jit(solution)/shard_map/all_to_all | solution.py:233
  176.0 1.4 add_convert_fusion.1
  178.2 1.7 collective-permute-start.1
  179.8 1.7 add_convert_fusion
  181.6 1.5 collective-permute-start.5
  183.2 1.1 all-to-all-done.6
  184.4 9.7 %collective-permute-done.5 = bf16[608,384]{1,0:T(8,128)(2,1)S(1)} collective-permute-done((bf16[608,384]{1,0:T(8,128)(2,1)S(1)}, bf16[608,384]{1,0:T(8,128)(2,1)S(1)}, u32[]{:S(2)}, u32[]{:S(2)}) %collective-permute-start.5) | collective-permute-done | bytes 466976 | tf_op jit(solution)/shard_map/ppermute | solution.py:770
  194.2 1.5 collective-permute-start.6
  195.8 1.1 fusion.1
  198.1 12.7 %weights.1 = (f32[384,1152]{1,0:T(8,128)}, f32[384,1152]{1,0:T(8,128)}, f32[384,384]{1,0:T(8,128)}, f32[384,384]{1,0:T(8,128)}, f32[384,1536]{1,0:T(8,128)}, /*i...) custom-call(bf16[48,4096]{1,0:T(8,128)(2,1)} %copy-done.5, ...), custom_call_target="tpu_custom_call" | custom-call | tf_op jit(solution)/shard_map/weights/pallas_call | solution.py:995
  211.4 1.1 pad_maximum_fusion.refs_4_
  212.5 1.6 collective-permute-start.7
  214.1 1.1 pad_maximum_fusion.1.refs_2_
  217.1 17.9 %collective-permute-done.3.refs_3_ = bf16[2,576,384]{2,1,0:T(8,128)(2,1)S(1)} collective-permute-done((bf16[2,576,384]{2,1,0:T(8,128)(2,1)S(1)}, bf16[2,576,384]{2,1,0:T(8,128)(2,1)S(1)}, u32[]{:S(2)}, u32[]{:S(2)}) %collective-permute-start.3) | collective-permute-done | bytes 884768 | tf_op jit(solution)/shard_map/ppermute | solution.py:770
  235.0 1.0 copy-done.8
  236.2 8.5 %errors.1 = (f32[384,1152]{1,0:T(8,128)}, f32[384,384]{1,0:T(8,128)}, f32[384,1536]{1,0:T(8,128)}, f32[4,384,384]{2,1,0:T(8,128)}, f32[96,384]{1,0:T(8,128)}) custom-call(s32[1]{0:T(128)} %bitcast.10.me_ref.refs_0_, bf16[48,4096]{1,0:T(8,128)(2,1)} %copy-done.5, bf16[2,576,384]{2,1,0:T(8,128)(2,1)} %copy-done.3, bf16[2,576,384]{2,1,0:T(8,128)(2,1)} %copy-done.9, ...), custom_call_target="tpu_custom_call" | custom-call | tf_op jit(solution)/shard_map/errors/pallas_call | solution.py:1024
  (96 shorter events, 17.2 us)
Async XLA Ops:
  1.8 19.0 %copy-start.11 = (s32[1,512]{1,0:T(1,128)S(1)}, s32[1,512]{1,0:T(1,128)}, u32[]{:S(2)}) copy-start(s32[1,512]{1,0:T(1,128)} %refs_2_.3) | copy-start | bytes 6148
  1.8 19.9 %copy-start.13 = (s32[64,16]{0,1:T(8,128)S(1)}, s32[64,16]{0,1:T(8,128)}, u32[]{:S(2)}) copy-start(s32[64,16]{0,1:T(8,128)} %param.31) | copy-start | bytes 12292
  1.8 19.9 %copy-start.14 = (s32[64]{0:T(128)S(1)}, s32[64]{0:T(128)}, u32[]{:S(2)}) copy-start(s32[64]{0:T(128)} %param.32) | copy-start | bytes 772
  13.3 25.6 %all-to-all-start = ((bf16[32,64,96]{2,1,0:T(8,128)(2,1)}), bf16[32,64,96]{2,1,0:T(8,128)(2,1)S(1)}, u32[]{:S(2)}, u32[]{:S(2)}) async-start(bf16[32,64,96]{2,1,0:T(8,128)(2,1)} %broadcast_in_dim.94), calls=%async_computation | async-start | bytes 1048576 | tf_op jit(solution)/shard_map/all_to_all | solution.py:233
  22.2 16.6 %copy-start.12 = (s32[1,512]{1,0:T(1,128)S(1)}, s32[1,512]{1,0:T(1,128)}, u32[]{:S(2)}) copy-start(s32[1,512]{1,0:T(1,128)} %refs_2_.3) | copy-start | bytes 6148
  38.8 5.5 %copy-start.4 = (bf16[32,64,96]{2,1,0:T(8,128)(2,1)}, bf16[32,64,96]{2,1,0:T(8,128)(2,1)S(1)}, u32[]{:S(2)}) copy-start(bf16[32,64,96]{2,1,0:T(8,128)(2,1)S(1)} %all-to-all-done) | copy-start | bytes 1179652
  45.8 13.1 %all-to-all-start.1 = ((f32[32,1,256]{2,1,0:T(1,128)}), f32[32,1,256]{2,1,0:T(1,128)S(1)}, u32[]{:S(2)}, u32[]{:S(2)}) async-start(f32[32,1,256]{2,1,0:T(1,128)} %reshape.315), calls=%async_computation.1 | async-start | bytes 65536 | tf_op jit(solution)/shard_map/all_to_all | solution.py:233
  61.0 2.2 copy-start.1
  63.2 1.0 copy-start.10
  65.9 31.5 %all-to-all-start.2 = ((f32[32,64,96]{2,1,0:T(8,128)}), f32[32,64,96]{2,1,0:T(8,128)S(1)}, u32[]{:S(2)}, u32[]{:S(2)}) async-start(f32[32,64,96]{2,1,0:T(8,128)} %bitcast.16), calls=%async_computation.2 | async-start | bytes 2097152 | tf_op jit(solution)/shard_map/all_to_all | solution.py:908
  97.4 1.0 copy-start
  119.5 22.4 %copy-start.6 = (bf16[4,576,384]{2,1,0:T(8,128)(2,1)S(1)}, bf16[4,576,384]{2,1,0:T(8,128)(2,1)}, u32[]{:S(2)}) copy-start(bf16[4,576,384]{2,1,0:T(8,128)(2,1)} %get-tuple-element.168) | copy-start | bytes 5308420
  134.2 10.8 %all-to-all-start.4 = ((f32[32,8,128]{2,1,0:T(8,128)}), f32[32,8,128]{2,1,0:T(8,128)S(1)}, u32[]{:S(2)}, u32[]{:S(2)}) async-start(f32[32,8,128]{2,1,0:T(8,128)} %broadcast_in_dim.105), calls=%async_computation.4 | async-start | bytes 262144 | tf_op jit(solution)/shard_map/all_to_all | solution.py:233
  140.2 39.6 %collective-permute-start.4 = (bf16[2,608,384]{2,1,0:T(8,128)(2,1)}, bf16[2,608,384]{2,1,0:T(8,128)(2,1)}, u32[]{:S(2)}, u32[]{:S(2)}) collective-permute-start(bf16[2,608,384]{2,1,0:T(8,128)(2,1)} %slice.68), channel_id=1, source_target_pairs={{0,16},{8,24},{16,0},{24,8},{1,17},{9,25},{17,1},{25,9},{2,18},{10... | collective-permute-start | bytes 2801672 | tf_op jit(solution)/shard_map/ppermute | solution.py:770
  142.9 33.1 %collective-permute-start = (bf16[2,576,384]{2,1,0:T(8,128)(2,1)}, bf16[2,576,384]{2,1,0:T(8,128)(2,1)}, u32[]{:S(2)}, u32[]{:S(2)}) collective-permute-start(bf16[2,576,384]{2,1,0:T(8,128)(2,1)} %slice.64), channel_id=1, source_target_pairs={{0,8},{8,0},{16,24},{24,16},{1,9},{9,1},{17,25},{25,17},{2,10},{10... | collective-permute-start | bytes 2654216 | tf_op jit(solution)/shard_map/ppermute | solution.py:770
  145.0 0.6 copy-start.7
  161.3 11.4 %all-to-all-start.5 = ((f32[32,8,128]{2,1,0:T(8,128)}), f32[32,8,128]{2,1,0:T(8,128)S(1)}, u32[]{:S(2)}, u32[]{:S(2)}) async-start(f32[32,8,128]{2,1,0:T(8,128)} %bitcast.147), calls=%async_computation.5 | async-start | bytes 262144 | tf_op jit(solution)/shard_map/all_to_all | solution.py:240
  173.4 10.8 %all-to-all-start.6 = ((f32[32,8,128]{2,1,0:T(8,128)}), f32[32,8,128]{2,1,0:T(8,128)S(1)}, u32[]{:S(2)}, u32[]{:S(2)}) async-start(f32[32,8,128]{2,1,0:T(8,128)} %broadcast_in_dim.106), calls=%async_computation.6 | async-start | bytes 262144 | tf_op jit(solution)/shard_map/all_to_all | solution.py:233
  178.2 17.6 %collective-permute-start.1 = (bf16[576,384]{1,0:T(8,128)(2,1)}, bf16[576,384]{1,0:T(8,128)(2,1)}, u32[]{:S(2)}, u32[]{:S(2)}) collective-permute-start(bf16[576,384]{1,0:T(8,128)(2,1)} %slice_bitcast_fusion.2), channel_id=1, source_target_pairs={{0,16},{8,24},{16,0},{24,8},{1,17},{9,25},{17,1},{25,9},{2,18},{10... | collective-permute-start | bytes 1327112 | tf_op jit(solution)/shard_map/ppermute | solution.py:770
  181.6 12.5 %collective-permute-start.5 = (bf16[608,384]{1,0:T(8,128)(2,1)S(1)}, bf16[608,384]{1,0:T(8,128)(2,1)S(1)}, u32[]{:S(2)}, u32[]{:S(2)}) collective-permute-start(bf16[608,384]{1,0:T(8,128)(2,1)S(1)} %slice_bitcast_fusion), channel_id=1, source_target_pairs={{0,8},{8,0},{16,24},{24,16},{1,9},{9,1},{17,25},{25,17},{2,10},{10... | collective-permute-start | bytes 1400840 | tf_op jit(solution)/shard_map/ppermute | solution.py:770
  184.4 13.7 %copy-start.5 = (bf16[48,4096]{1,0:T(8,128)(2,1)}, bf16[48,4096]{1,0:T(8,128)(2,1)S(1)}, u32[]{:S(2)}) copy-start(bf16[48,4096]{1,0:T(8,128)(2,1)S(1)} %constant_dynamic-update-slice_fusion.refs_0_.refs_1_) | copy-start | bytes 1179652
  194.2 17.1 %collective-permute-start.6 = (bf16[608,384]{1,0:T(8,128)(2,1)S(1)}, bf16[608,384]{1,0:T(8,128)(2,1)}, u32[]{:S(2)}, u32[]{:S(2)}) collective-permute-start(bf16[608,384]{1,0:T(8,128)(2,1)S(1)} %fusion), channel_id=1, source_target_pairs={{0,8},{8,0},{16,24},{24,16},{1,9},{9,1},{17,25},{25,17},{2,10},{10... | collective-permute-start | bytes 1400840 | tf_op jit(solution)/shard_map/ppermute | solution.py:770
  196.9 17.2 %collective-permute-start.2 = (bf16[576,384]{1,0:T(8,128)(2,1)S(1)}, bf16[576,384]{1,0:T(8,128)(2,1)}, u32[]{:S(2)}, u32[]{:S(2)}) collective-permute-start(bf16[576,384]{1,0:T(8,128)(2,1)S(1)} %fusion.1), channel_id=1, source_target_pairs={{0,16},{8,24},{16,0},{24,8},{1,17},{9,25},{17,1},{25,9},{2,18},{10... | collective-permute-start | bytes 1327112 | tf_op jit(solution)/shard_map/ppermute | solution.py:770
  212.5 23.5 %copy-start.2 = (bf16[2,608,384]{2,1,0:T(8,128)(2,1)}, bf16[2,608,384]{2,1,0:T(8,128)(2,1)S(1)}, u32[]{:S(2)}) copy-start(bf16[2,608,384]{2,1,0:T(8,128)(2,1)S(1)} %pad_maximum_fusion.refs_4_) | copy-start | bytes 2801668
  212.5 22.5 %collective-permute-start.7 = (bf16[2,608,384]{2,1,0:T(8,128)(2,1)S(1)}, bf16[2,608,384]{2,1,0:T(8,128)(2,1)S(1)}, u32[]{:S(2)}, u32[]{:S(2)}) collective-permute-start(bf16[2,608,384]{2,1,0:T(8,128)(2,1)S(1)} %pad_maximum_fusion.refs_4_), channel_id=1, source_target_pairs={{0,16},{8,24},{16,0},{24,8},{1,17},{9,25},{17,1},{25,9},{2,18},{10... | collective-permute-start | bytes 2801672 | tf_op jit(solution)/shard_map/ppermute | solution.py:770
  215.2 20.8 %copy-start.3 = (bf16[2,576,384]{2,1,0:T(8,128)(2,1)}, bf16[2,576,384]{2,1,0:T(8,128)(2,1)S(1)}, u32[]{:S(2)}) copy-start(bf16[2,576,384]{2,1,0:T(8,128)(2,1)S(1)} %pad_maximum_fusion.1.refs_2_) | copy-start | bytes 2654212
  215.2 19.8 %collective-permute-start.3 = (bf16[2,576,384]{2,1,0:T(8,128)(2,1)S(1)}, bf16[2,576,384]{2,1,0:T(8,128)(2,1)S(1)}, u32[]{:S(2)}, u32[]{:S(2)}) collective-permute-start(bf16[2,576,384]{2,1,0:T(8,128)(2,1)S(1)} %pad_maximum_fusion.1.refs_2_), channel_id=1, source_target_pairs={{0,8},{8,0},{16,24},{24,16},{1,9},{9,1},{17,25},{25,17},{2,10},{10... | collective-permute-start | bytes 2654216 | tf_op jit(solution)/shard_map/ppermute | solution.py:770
  235.0 1.2 copy-start.9
  235.0 1.0 copy-start.8
where the time goes:
time: 250 us; the launch traced here: 246 us
  Pallas kernels  106 us (42%)
  waiting for transfers between devices  41.9 us (17%)
  starting transfers between devices  35 us (14%)
  local copies, waits for them, and re-layouts  18.5 us (7%)
  other arithmetic  17.7 us (7%)
  blocking collectives  14 us (6%)
  matrix products  9.68 us (4%)
  between operations  3.13 us (1%)
    pallas_call x2, Pallas kernels, backward_call(): pl.pallas_call(backward_kernel, out_shape=outs + [jax.ShapeDtypeStruct((1...  31.3 us
    ppermute x8, waiting for transfers between devices, exchange(): return lax.ppermute(value, 'stream', [(i, i ^ turn) for i in range(4)])  27.6 us
    pallas_call x2, Pallas kernels, encode_call(): pl.pallas_call(lambda *refs: encode_kernel(first, *refs), out_shape=outs,...  26.3 us
    all_to_all x4, starting transfers between devices, spread(): return lax.all_to_all(copies, AXES, 0, 0, tiled=True)  18.5 us
    all_to_all x1, blocking collectives, all_sum(): got = lax.all_to_all(pieces, AXES, 0, 0, tiled=True)  14 us
    pallas_call x1, Pallas kernels, shards(): pl.pallas_call(grads_kernel, grid_spec=pltpu.PrefetchScalarGridSpec(num_s...  13 us
    pallas_call x1, Pallas kernels, shards(): pl.pallas_call(lambda *refs: weight_kernel(spans, rate, *refs), grid=(ste...  12.7 us
    pallas_call x1, Pallas kernels, shards(): pl.pallas_call(lambda *refs: factors_kernel(bounds, *refs), grid_spec=plt...  11.1 us
  transfers between devices with their start and end apart: 14, of which 6 were waited for; matrix products, arithmetic and copies ran while one was open for 10% of the time, Pallas kernels for 27%

commit v1 on v0

--- a/solution.py
+++ b/solution.py
@@ -9,46 +9,14 @@
 from jax.sharding import PartitionSpec as P
 
 D = 384
-HEADS = 12
 HDIM = 32
 FF = 1536
 NSEG = 4
 
 
-HIGH = lax.Precision.HIGHEST
 SOFT = 0.03
 MOMENTUM = 0.9
 RATE = 0.1
-
-
-def split_vec(packed):
-    return jnp.split(
-        packed,
-        [3 * D, 4 * D, 4 * D + FF, 5 * D + FF, 6 * D + FF, 7 * D + FF, 8 * D + FF, 9 * D + FF],
-    )
-
-
-def inner(first, second):
-    return lax.dot_general(
-        first, second, (((0,), (0,)), ((), ())), preferred_element_type=jnp.float32
-    )
-
-
-def layer_norm(resid, gain, shift):
-    center = resid - jnp.mean(resid, -1, keepdims=True)
-    inv_std = lax.rsqrt(jnp.mean(center * center, -1, keepdims=True) + 1e-05)
-    normed = center * inv_std
-    return (normed * gain + shift, normed, inv_std)
-
-
-def norm_back(grad_out, gain, normed, inv_std):
-    scaled = grad_out * gain
-    grad_in = inv_std * (
-        scaled
-        - jnp.mean(scaled, -1, keepdims=True)
-        - normed * jnp.mean(scaled * normed, -1, keepdims=True)
-    )
-    return (grad_in, jnp.sum(grad_out * normed, 0), jnp.sum(grad_out, 0))
 
 
 def gelu(value):
@@ -62,169 +30,6 @@
     )
 
 
-def rotary(value, cosine, sine):
-    half = value.shape[-1] // 2
-    return value * cosine + jnp.concatenate([-value[..., half:], value[..., :half]], -1) * sine
-
-
-def rotary_back(grad, cosine, sine):
-    half = grad.shape[-1] // 2
-    turned = grad * sine
-    return grad * cosine + jnp.concatenate([turned[..., half:], -turned[..., :half]], -1)
-
-
-def tables(segment):
-    count = segment.shape[0]
-    places = jnp.arange(count)
-    same = segment[:, None] == segment[None, :]
-    position = jnp.sum(same & (places[None, :] < places[:, None]), 1).astype(jnp.float32)
-    freqs = 10000.0 ** (-(jnp.arange(HDIM // 2).astype(jnp.float32) * 2.0) / HDIM)
-    angle = position[:, None] * freqs[None, :]
-    cosine = jnp.concatenate([jnp.cos(angle), jnp.cos(angle)], -1)[:, None, :]
-    sine = jnp.concatenate([jnp.sin(angle), jnp.sin(angle)], -1)[:, None, :]
-    return (same, cosine, sine)
-
-
-def encode(tokens_in, same, cosine, sine, mats, packed):
-    w_qkv, w_out, w_up, w_down, w_head = mats
-    b_qkv, b_out, b_up, b_down, gain_one, shift_one, gain_two, shift_two, b_head = split_vec(packed)
-    count = tokens_in.shape[0]
-    scale = HDIM ** (-0.5)
-    qkv = (jnp.dot(tokens_in, w_qkv, preferred_element_type=jnp.float32) + b_qkv).reshape(
-        count, 3, HEADS, HDIM
-    )
-    queries = rotary(qkv[:, 0], cosine, sine).astype(jnp.bfloat16)
-    keys_rot = rotary(qkv[:, 1], cosine, sine).astype(jnp.bfloat16)
-    values = qkv[:, 2].astype(jnp.bfloat16)
-    scores = (
-        jnp.einsum("ihd,jhd->hij", queries, keys_rot, preferred_element_type=jnp.float32) * scale
-    )
-    scores = jnp.where(same[None], scores, -1e30)
-    expo = jnp.exp(scores - jnp.max(scores, -1, keepdims=True))
-    probs = expo / jnp.sum(expo, -1, keepdims=True)
-    probs_low = probs.astype(jnp.bfloat16)
-    context = (
-        jnp.einsum("hij,jhd->ihd", probs_low, values, preferred_element_type=jnp.float32)
-        .reshape(count, D)
-        .astype(jnp.bfloat16)
-    )
-    attended = jnp.dot(context, w_out, preferred_element_type=jnp.float32) + b_out
-    hidden_one, normed_one, inv_one = layer_norm(
-        tokens_in.astype(jnp.float32) + attended, gain_one, shift_one
-    )
-    hidden_low = hidden_one.astype(jnp.bfloat16)
-    pre_act = jnp.dot(hidden_low, w_up, preferred_element_type=jnp.float32) + b_up
-    act_low = gelu(pre_act).astype(jnp.bfloat16)
-    mixed = jnp.dot(act_low, w_down, preferred_element_type=jnp.float32) + b_down
-    hidden_two, normed_two, inv_two = layer_norm(hidden_one + mixed, gain_two, shift_two)
-    second_low = hidden_two.astype(jnp.bfloat16)
-    emitted = jnp.dot(second_low, w_head, preferred_element_type=jnp.float32) + b_head
-    inv_len = lax.rsqrt(jnp.sum(emitted * emitted, -1, keepdims=True) + 1e-06)
-    output = emitted * inv_len
-    kept = (
-        queries,
-        keys_rot,
-        values,
-        probs,
-        probs_low,
-        context,
-        normed_one,
-        inv_one,
-        hidden_low,
-        pre_act,
-        act_low,
-        normed_two,
-        inv_two,
-        second_low,
-        inv_len,
-        output,
-    )
-    return (output, kept)
-
-
-def backward(grad_vec, tokens_in, cosine, sine, kept, mats, packed):
-    w_qkv, w_out, w_up, w_down, w_head = mats
-    b_qkv, b_out, b_up, b_down, gain_one, shift_one, gain_two, shift_two, b_head = split_vec(packed)
-    (
-        queries,
-        keys_rot,
-        values,
-        probs,
-        probs_low,
-        context,
-        normed_one,
-        inv_one,
-        hidden_low,
-        pre_act,
-        act_low,
-        normed_two,
-        inv_two,
-        second_low,
-        inv_len,
-        output,
-    ) = kept
-    count = tokens_in.shape[0]
-    scale = HDIM ** (-0.5)
-    grad_emit = inv_len * (grad_vec - output * jnp.sum(grad_vec * output, -1, keepdims=True))
-    emit_low = grad_emit.astype(jnp.bfloat16)
-    grad_hidden_two = jnp.dot(emit_low, w_head.T, preferred_element_type=jnp.float32)
-    grad_resid_two, grad_gain_two, grad_shift_two = norm_back(
-        grad_hidden_two, gain_two, normed_two, inv_two
-    )
-    mixed_low = grad_resid_two.astype(jnp.bfloat16)
-    grad_act = jnp.dot(mixed_low, w_down.T, preferred_element_type=jnp.float32)
-    grad_pre = grad_act * gelu_slope(pre_act)
-    pre_low = grad_pre.astype(jnp.bfloat16)
-    grad_hidden_one = grad_resid_two + jnp.dot(pre_low, w_up.T, preferred_element_type=jnp.float32)
-    grad_resid_one, grad_gain_one, grad_shift_one = norm_back(
-        grad_hidden_one, gain_one, normed_one, inv_one
-    )
-    attn_low = grad_resid_one.astype(jnp.bfloat16)
-    grad_context = (
-        jnp.dot(attn_low, w_out.T, preferred_element_type=jnp.float32)
-        .reshape(count, HEADS, HDIM)
-        .astype(jnp.bfloat16)
-    )
-    grad_probs = jnp.einsum(
-        "ihd,jhd->hij", grad_context, values, preferred_element_type=jnp.float32
-    )
-    grad_values = jnp.einsum(
-        "hij,ihd->jhd", probs_low, grad_context, preferred_element_type=jnp.float32
-    )
-    grad_scores = probs * (grad_probs - jnp.sum(grad_probs * probs, -1, keepdims=True))
-    scores_low = grad_scores.astype(jnp.bfloat16)
-    grad_queries = (
-        jnp.einsum("hij,jhd->ihd", scores_low, keys_rot, preferred_element_type=jnp.float32) * scale
-    )
-    grad_keys = (
-        jnp.einsum("hij,ihd->jhd", scores_low, queries, preferred_element_type=jnp.float32) * scale
-    )
-    grad_queries = rotary_back(grad_queries, cosine, sine)
-    grad_keys = rotary_back(grad_keys, cosine, sine)
-    grad_qkv_act = jnp.stack([grad_queries, grad_keys, grad_values], 1).reshape(count, 3 * D)
-    grad_packed = jnp.concatenate(
-        [
-            jnp.sum(grad_qkv_act, 0),
-            jnp.sum(grad_resid_one, 0),
-            jnp.sum(grad_pre, 0),
-            jnp.sum(grad_resid_two, 0),
-            grad_gain_one,
-            grad_shift_one,
-            grad_gain_two,
-            grad_shift_two,
-            jnp.sum(grad_emit, 0),
-        ]
-    )
-    pairs = (
-        (tokens_in, grad_qkv_act.astype(jnp.bfloat16)),
-        (context, attn_low),
-        (hidden_low, pre_low),
-        (act_low, mixed_low),
-        (second_low, emit_low),
-    )
-    return (pairs, grad_packed)
-
-
 AXES = ("stream", "replica")
 
 
@@ -233,14 +38,16 @@
     return lax.all_to_all(copies, AXES, 0, 0, tiled=True)
 
 
-def all_sum(value):
+def sum_piece(value):
     count = lax.axis_size("stream") * lax.axis_size("replica")
     rows, cols = value.shape
     pieces = value.reshape(rows, count, cols // count).transpose(1, 0, 2)
-    got = lax.all_to_all(pieces, AXES, 0, 0, tiled=True)
-    mine = jnp.sum(got, 0)
-    back = spread(mine, count)
-    return back.transpose(1, 0, 2).reshape(rows, cols)
+    return jnp.sum(lax.all_to_all(pieces, AXES, 0, 0, tiled=True), 0)
+
+
+def join_pieces(mine):
+    count = lax.axis_size("stream") * lax.axis_size("replica")
+    return spread(mine, count).transpose(1, 0, 2).reshape(mine.shape[0], -1)
 
 
 def thirds(value):
@@ -422,7 +229,7 @@
     lax.fori_loop(0, count // tile, rest, 0)
 
 
-def encode_call(tokens, segment, table, weights, vectors, first, name):
+def encode_call(tokens, segment, table, weights, vectors, first):
     count = tokens.shape[0]
     f32, low = jnp.float32, jnp.bfloat16
     shapes = [
@@ -433,14 +240,14 @@
     if first:
         outs += [jax.ShapeDtypeStruct(w.shape, low) for w in weights]
     return pl.pallas_call(
-        lambda *refs: encode_kernel(first, *refs), out_shape=outs, name=name
+        lambda *refs: encode_kernel(first, *refs), out_shape=outs
     )(tokens, segment[:, None], segment[None, :], table, *weights, vectors)
 
 
 def backward_kernel(*refs):
     (
         grad_ref, segc_ref, segr_ref, q_ref, k_ref, v_ref, n1_ref, pre_ref, n2_ref, out_ref,
-        stat_ref, cos_ref, sin_ref, wqkv_ref, wout_ref, wup_ref, wdown_ref, whead_ref, vec_ref,
+        stat_ref, cos_ref, sin_ref, _, wout_ref, wup_ref, wdown_ref, whead_ref, vec_ref,
     ) = refs[:19]
     yqkv_ref, yout_ref, yup_ref, ydown_ref, yhead_ref, packed_ref = refs[19:25]
     dk_ref, dv_ref, p_ref, s_ref, c_ref = refs[25:]
@@ -545,7 +352,7 @@
     lax.fori_loop(0, count // tile, last, 0)
 
 
-def backward_call(grad, segment, kept, weights, vectors, name):
+def backward_call(grad, segment, kept, weights, vectors):
     q, k, v, _, n1, _, pre, _, n2, _, out, _, stat, cosine, sine = kept
     count = q.shape[0]
     tile = min(count, TILE)
@@ -561,7 +368,6 @@
             pltpu.VMEM((4 * tile, count), low),
             pltpu.VMEM((8 * tile, 128), low),
         ],
-        name=name,
     )(
         grad, segment[:, None], segment[None, :], q, k, v, n1, pre, n2, out, stat, cosine, sine,
         *weights, vectors,
@@ -770,19 +576,8 @@
     return lax.ppermute(value, "stream", [(i, i ^ turn) for i in range(4)])
 
 
-def stream_sum(a, b):
-    def add(first, second):
-        return (first.astype(jnp.float32) + second.astype(jnp.float32)).astype(jnp.bfloat16)
-
-    both = []
-    got = [exchange(a[2:], 1), exchange(b[2:], 2)]
-    half = [add(a[:2], got[0]), add(b[:2], got[1])]
-    got = [exchange(half[0][1], 2), exchange(half[1][1], 1)]
-    full = [add(half[0][0], got[0]), add(half[1][0], got[1])]
-    got = [exchange(full[0], 2), exchange(full[1], 1)]
-    pair = [jnp.stack([one, two], 0) for one, two in zip(full, got)]
-    last = [exchange(pair[0], 1), exchange(pair[1], 2)]
-    return pair[0], last[0], pair[1], last[1]
+def add(first, second):
+    return (first.astype(jnp.float32) + second.astype(jnp.float32)).astype(jnp.bfloat16)
 
 
 def shards(
@@ -831,16 +626,14 @@
     query_seg = jnp.arange(qtok, dtype=jnp.int32) // qlen
     *query_kept, m0, m1, m2, m3, m4 = encode_call(
         query_in, query_seg, table, weights, vec_row,
-        True, "encode_queries",
+        True,
     )
     mats = (m0, m1, m2, m3, m4)
     all_query = spread(query_kept[11], devices)
 
     doc_in = doc_embeds[0]
     doc_seg = doc_segments[0]
-    doc_kept = encode_call(
-        doc_in, doc_seg, table, mats, vec_row, False, "encode_documents"
-    )
+    doc_kept = encode_call(doc_in, doc_seg, table, mats, vec_row, False)
     doc_low = doc_kept[11]
     pdim = doc_low.shape[1]
 
@@ -908,12 +701,8 @@
     query_local = lax.all_to_all(query_grad, AXES, 0, 0, tiled=True)
     doc_grad = jnp.dot(sim_low, rows_all, preferred_element_type=jnp.float32)
 
-    *doc_out, doc_packed = backward_call(
-        doc_grad, doc_seg, doc_kept, mats, vec_row, "backward_documents"
-    )
-    *query_out, query_packed = backward_call(
-        query_local, query_seg, query_kept, mats, vec_row, "backward_queries"
-    )
+    *doc_out, doc_packed = backward_call(doc_grad, doc_seg, doc_kept, mats, vec_row)
+    *query_out, query_packed = backward_call(query_local, query_seg, query_kept, mats, vec_row)
     inputs = ((doc_in, query_in),) + tuple((doc_kept[n], query_kept[n]) for n in (3, 5, 7, 9))
     acts = [
         v for (dx, qx), dy, qy in zip(inputs, doc_out, query_out) for v in (dx, qx, dy, qy)
@@ -923,8 +712,8 @@
         edges.append(edges[-1] + m)
     bounds = list(zip(edges[:-1], edges[1:]))
     side = doc_packed.shape[1] // 8
-    full = edges[-1] + side
-    full += -full % (128 * devices) if devices <= 32 else -full % (16 * devices)
+    span = edges[-1] + side
+    span += -span % (128 * devices) if devices <= 32 else -span % (16 * devices)
     a_grads, b_grads, left = pl.pallas_call(
         grads_kernel,
         grid_spec=pltpu.PrefetchScalarGridSpec(
@@ -934,19 +723,23 @@
             out_specs=[
                 pl.BlockSpec((4, 576, D), lambda i, me: (0, 0, 0)),
                 pl.BlockSpec((4, 608, D), lambda i, me: (0, 0, 0)),
-                pl.BlockSpec((8, full), lambda i, me: (0, 0)),
+                pl.BlockSpec((8, span), lambda i, me: (0, 0)),
             ],
         ),
         out_shape=[
             jax.ShapeDtypeStruct((4, 576, D), jnp.bfloat16),
             jax.ShapeDtypeStruct((4, 608, D), jnp.bfloat16),
-            jax.ShapeDtypeStruct((8, full), jnp.float32),
+            jax.ShapeDtypeStruct((8, span), jnp.float32),
         ],
         name="grads",
     )(me_stream, *acts, fac_parts, early, doc_packed, query_packed)
-    sums = stream_sum(a_grads, b_grads)
-
-    summed = all_sum(left)
+    got = [exchange(a_grads[2:], 1), exchange(b_grads[2:], 2)]
+    half = [add(a_grads[:2], got[0]), add(b_grads[:2], got[1])]
+
+    summed = join_pieces(sum_piece(left))
+    summed, half = lax.optimization_barrier((summed, half))
+    got = [exchange(half[0][1], 2), exchange(half[1][1], 1)]
+    full = [add(half[0][0], got[0]), add(half[1][0], got[1])]
 
     wide += -wide % (128 * devices) if devices <= 32 else -wide % (128 * devices // 8)
     basis, right = pl.pallas_call(
@@ -972,7 +765,14 @@
         ],
         name="factors",
     )(me_stream, summed, *acts, *errs)
-    joined = all_sum(right)
+    right, full = lax.optimization_barrier((right, full))
+    got = [exchange(full[0], 2), exchange(full[1], 1)]
+    mine = sum_piece(right)
+    pair = [jnp.stack([one, two], 0) for one, two in zip(full, got)]
+    mine, pair = lax.optimization_barrier((mine, pair))
+    last = [exchange(pair[0], 1), exchange(pair[1], 2)]
+    joined = join_pieces(mine)
+    sums = (pair[0], last[0], pair[1], last[1])
     rights, spans, at = [], [], 0
     for _, n in sizes:
         rights.append(joined[:, at : at + n])

time: 250 us -> 249 us (level)
  blocking collectives: 14 us -> 0 us
  waiting for transfers between devices: 41.9 us -> 52.3 us
  starting transfers between devices: 35 us -> 40 us
    all_to_all x1 -> x2, waiting for transfers between devices: 5.32 us -> 25.8 us  [sum_piece(): return jnp.sum(lax.all_to_all(pieces, AXES, 0, 0, tiled=True), 0)]
    ppermute x8, waiting for transfers between devices: 27.6 us -> 12.7 us  [exchange(): return lax.ppermute(value, 'stream', [(i, i ^ turn) for i in range(4)])]
    all_to_all x1 -> x0, blocking collectives: 14 us -> none  [all_sum(): got = lax.all_to_all(pieces, AXES, 0, 0, tiled=True)]
    all_to_all x4, waiting for transfers between devices: 8.98 us -> 13.8 us  [spread(): return lax.all_to_all(copies, AXES, 0, 0, tiled=True)]
    all_to_all x1 -> x2, starting transfers between devices: 3.25 us -> 6.4 us  [sum_piece(): return jnp.sum(lax.all_to_all(pieces, AXES, 0, 0, tiled=True), 0)]
  transfers between devices with their start and end apart: 14 -> 15, of which waited for: 6 -> 8; matrix products, arithmetic and copies ran while one was open for 10% -> 7% of each run, Pallas kernels for 27% -> 23%
where the time goes in v1:
time: 249 us; the launch traced here: 246 us
  Pallas kernels  106 us (43%)
  waiting for transfers between devices  52.3 us (21%)
  starting transfers between devices  40 us (16%)
  local copies, waits for them, and re-layouts  18.1 us (7%)
  other arithmetic  16.6 us (7%)
  matrix products  9.67 us (4%)
  between operations  3.17 us (1%)
    pallas_call x2, Pallas kernels, backward_call(): pl.pallas_call(backward_kernel, out_shape=outs + [jax.ShapeDtypeStruct((1...  31.3 us
    pallas_call x2, Pallas kernels, encode_call(): pl.pallas_call(lambda *refs: encode_kernel(first, *refs), out_shape=outs)  26.3 us
    all_to_all x2, waiting for transfers between devices, sum_piece(): return jnp.sum(lax.all_to_all(pieces, AXES, 0, 0, tiled=True), 0)  25.8 us
    all_to_all x4, starting transfers between devices, spread(): return lax.all_to_all(copies, AXES, 0, 0, tiled=True)  20.7 us
    all_to_all x4, waiting for transfers between devices, spread(): return lax.all_to_all(copies, AXES, 0, 0, tiled=True)  13.8 us
    pallas_call x1, Pallas kernels, shards(): pl.pallas_call(grads_kernel, grid_spec=pltpu.PrefetchScalarGridSpec(num_s...  13 us
    ppermute x8, waiting for transfers between devices, exchange(): return lax.ppermute(value, 'stream', [(i, i ^ turn) for i in range(4)])  12.7 us
    pallas_call x1, Pallas kernels, shards(): pl.pallas_call(lambda *refs: weight_kernel(spans, rate, *refs), grid=(ste...  12.7 us
  transfers between devices with their start and end apart: 15, of which 8 were waited for; matrix products, arithmetic and copies ran while one was open for 7% of the time, Pallas kernels for 23%

profile of v1, /device:TPU:0, one launch (start us, length us, event | category | flops | bytes accessed | tf_op | source)
XLA Modules:
  0.0 245.8 jit_solution(8906905489502275853)
XLA Ops:
  1.8 9.8 %shard_map.443 = (bf16[64,384]{1,0:T(8,128)(2,1)}, bf16[64,384]{1,0:T(8,128)(2,1)}, bf16[64,384]{1,0:T(8,128)(2,1)}, bf16[64,384]{1,0:T(8,128)(2,1)}, f32[64,384...) custom-call(bf16[64,384]{1,0:T(8,128)(2,1)} %bitcast.139, ...), custom_call_target="tpu_custom_call" | custom-call | tf_op jit(solution)/shard_map/pallas_call | solution.py:242
  11.6 1.6 broadcast_in_dim.94
  13.3 7.5 %all-to-all-start = ((bf16[32,64,96]{2,1,0:T(8,128)(2,1)}), bf16[32,64,96]{2,1,0:T(8,128)(2,1)S(1)}, u32[]{:S(2)}, u32[]{:S(2)}) async-start(bf16[32,64,96]{2,1,0:T(8,128)(2,1)} %broadcast_in_dim.94), calls=%async_computation | async-start | bytes 1048576 | tf_op jit(solution)/shard_map/all_to_all | solution.py:38
  20.8 0.9 copy.93.refs_1_
  22.3 16.4 %shard_map.444 = (bf16[512,384]{1,0:T(8,128)(2,1)}, bf16[512,384]{1,0:T(8,128)(2,1)}, bf16[512,384]{1,0:T(8,128)(2,1)}, bf16[512,384]{1,0:T(8,128)(2,1)}, f32[51...) custom-call(bf16[512,384]{1,0:T(8,128)(2,1)} %bitcast.115, ...), custom_call_target="tpu_custom_call" | custom-call | tf_op jit(solution)/shard_map/pallas_call | solution.py:242
  38.8 5.5 %select_reduce_fusion.3 = (f32[2048]{0:T(1024)S(1)}, f32[2048]{0:T(1024)S(1)}, f32[2048]{0:T(1024)S(1)}, f32[2048]{0:T(1024)S(1)}, f32[512,2048]{1,0:T(8,128)}) fusion(pred[512]{0:T(512)(128)(4,1)S(1)} %get-tuple-element.208, pred[512]{0:T(512)(128)(4,1)S(1)} %get-tuple-element.206, pred[512]{0:T(512)(128)(4,1)S(1)} %get-tuple-element.207, ...), kind=kOutput, calls=%fused_computation.5 | convolution fusion | flops 210755584 | bytes 4720640 | tf_op jit(solution)/shard_map/dot_general | solution.py:644
  45.8 5.8 %all-to-all-start.1 = ((f32[32,1,256]{2,1,0:T(1,128)}), f32[32,1,256]{2,1,0:T(1,128)S(1)}, u32[]{:S(2)}, u32[]{:S(2)}) async-start(f32[32,1,256]{2,1,0:T(1,128)} %reshape.315), calls=%async_computation.1 | async-start | bytes 65536 | tf_op jit(solution)/shard_map/all_to_all | solution.py:38
  51.7 7.2 %all-to-all-done.1 = f32[32,1,256]{2,1,0:T(1,128)S(1)} async-done(((f32[32,1,256]{2,1,0:T(1,128)}), f32[32,1,256]{2,1,0:T(1,128)S(1)}, u32[]{:S(2)}, u32[]{:S(2)}) %all-to-all-start.1) | async-done | bytes 32800 | tf_op jit(solution)/shard_map/all_to_all | solution.py:38
  61.0 1.2 multiply_reduce_fusion
  62.2 0.9 copy-done.1
  63.1 1.0 multiply_convert_fusion
  64.2 1.7 fusion.17
  65.9 2.6 %all-to-all-start.2 = ((f32[32,64,96]{2,1,0:T(8,128)}), f32[32,64,96]{2,1,0:T(8,128)S(1)}, u32[]{:S(2)}, u32[]{:S(2)}) async-start(f32[32,64,96]{2,1,0:T(8,128)} %bitcast.16), calls=%async_computation.2 | async-start | bytes 2097152 | tf_op jit(solution)/shard_map/all_to_all | solution.py:701
  68.5 3.1 %early.1 = (f32[8,3072]{1,0:T(8,128)}, bf16[24,3552]{1,0:T(8,128)(2,1)}) custom-call(s32[1]{0:T(128)} %bitcast.10.me_ref.refs_0_, f32[8,1152]{1,0:T(8,128)} %bitcast.150, f32[8,384]{1,0:T(8,128)} %bitcast.156, f32[8,1536]{1,0:T(8,128)} %bitcast.149, f32[8,384]{1,0:T(8,128)} %bitcast.157, f32[8,96]{1,0:T(8,128)} %bitcast.158, f32[384,1152]{1,0:T(8,128)} %bitcast.104, ...), custom_call_target="tpu_custom_call" | custom-call | tf_op jit(solution)/shard_map/early/pallas_call | solution.py:659
  71.7 2.5 fusion.16.refs_0_
  74.1 23.3 %shard_map.445 = (bf16[512,1152]{1,0:T(8,128)(2,1)}, bf16[512,384]{1,0:T(8,128)(2,1)}, bf16[512,1536]{1,0:T(8,128)(2,1)}, bf16[512,384]{1,0:T(8,128)(2,1)}, bf16[512,96]{1,0:T(8,128)(2,1)}, /*index=5*/f32[1,5120]{1,0:T(1,128)}) custom-call(f32[512,96]{1,0:T(8,128)} %fusion.16.refs_0_, s32[512,1]{1,0:T(8,128)} %copy.93.refs_1_, s32[1,512]{1,0:T(1,128)} %refs_2_.3, ...), custom_call_target="tpu_custom_call" | custom-call | tf_op jit(solution)/shard_map/pallas_call | solution.py:361
  97.4 1.0 copy-done
  98.4 8.0 %shard_map.446 = (bf16[64,1152]{1,0:T(8,128)(2,1)}, bf16[64,384]{1,0:T(8,128)(2,1)}, bf16[64,1536]{1,0:T(8,128)(2,1)}, bf16[64,384]{1,0:T(8,128)(2,1)}, bf16[64,96]{1,0:T(8,128)(2,1)}, /*index=5*/f32[1,5120]{1,0:T(1,128)}) custom-call(f32[32,64,96]{2,1,0:T(8,128)} %copy-done, s32[64,1]{1,0:T(8,128)} %add_select_fusion.refs_1_, ...), custom_call_target="tpu_custom_call" | custom-call | tf_op jit(solution)/shard_map/pallas_call | solution.py:361
  106.4 13.0 %grads.1 = (bf16[4,576,384]{2,1,0:T(8,128)(2,1)}, bf16[4,608,384]{2,1,0:T(8,128)(2,1)}, f32[8,4096]{1,0:T(8,128)}) custom-call(s32[1]{0:T(128)} %bitcast.10.me_ref.refs_0_, bf16[512,384]{1,0:T(8,128)(2,1)} %bitcast.116, bf16[64,384]{1,0:T(8,128)(2,1)} %bitcast.140, bf16[512,1152]{1,0:T(8,128)(2,1)} %get-tuple-element.125.refs_2_.refs_4_, ...), custom_call_target="tpu_custom_call" | custom-call | tf_op jit(solution)/shard_map/grads/pallas_call | solution.py:717
  119.4 1.3 slice.59
  120.7 1.7 collective-permute-start
  122.4 1.3 slice.61
  123.7 1.6 collective-permute-start.1
  125.2 3.8 %all-to-all-start.3 = ((f32[32,8,128]{2,1,0:T(8,128)}), f32[32,8,128]{2,1,0:T(8,128)S(1)}, u32[]{:S(2)}, u32[]{:S(2)}) async-start(f32[32,8,128]{2,1,0:T(8,128)} %bitcast.29), calls=%async_computation.3 | async-start | bytes 262144 | tf_op jit(solution)/shard_map/all_to_all | solution.py:45
  130.3 17.3 %all-to-all-done.3 = f32[32,8,128]{2,1,0:T(8,128)S(1)} async-done(((f32[32,8,128]{2,1,0:T(8,128)}), f32[32,8,128]{2,1,0:T(8,128)S(1)}, u32[]{:S(2)}, u32[]{:S(2)}) %all-to-all-start.3) | async-done | bytes 131104 | tf_op jit(solution)/shard_map/all_to_all | solution.py:45
  148.3 4.8 %all-to-all-start.4 = ((f32[32,8,128]{2,1,0:T(8,128)}), f32[32,8,128]{2,1,0:T(8,128)S(1)}, u32[]{:S(2)}, u32[]{:S(2)}) async-start(f32[32,8,128]{2,1,0:T(8,128)} %broadcast_in_dim.105), calls=%async_computation.4 | async-start | bytes 262144 | tf_op jit(solution)/shard_map/all_to_all | solution.py:38
  153.1 1.7 add_convert_fusion.1
  154.7 1.4 add_convert_fusion
  156.2 5.1 %all-to-all-done.4 = f32[32,8,128]{2,1,0:T(8,128)S(1)} async-done(((f32[32,8,128]{2,1,0:T(8,128)}), f32[32,8,128]{2,1,0:T(8,128)S(1)}, u32[]{:S(2)}, u32[]{:S(2)}) %all-to-all-start.4) | async-done | bytes 131104 | tf_op jit(solution)/shard_map/all_to_all | solution.py:38
  161.9 11.1 %factors.1 = (f32[8,3072]{1,0:T(8,128)}, f32[8,4096]{1,0:T(8,128)}) custom-call(s32[1]{0:T(128)} %bitcast.10.me_ref.refs_0_, f32[8,4096]{1,0:T(8,128)} %bitcast.127, bf16[512,384]{1,0:T(8,128)(2,1)} %bitcast.117, bf16[64,384]{1,0:T(8,128)(2,1)} %bitcast.141, bf16[512,1152]{1,0:T(8,128)(2,1)} %get-tuple-element.125.refs_2_.refs_4_, ...), custom_call_target="tpu_custom_call" | custom-call | tf_op jit(solution)/shard_map/factors/pallas_call | solution.py:745
  173.0 1.5 constant_dynamic-update-slice_fusion.9
  174.5 1.5 constant_dynamic-update-slice_fusion.8
  176.0 1.5 constant_dynamic-update-slice_fusion.7
  177.6 0.9 collective-permute-start.3
  179.3 1.5 constant_dynamic-update-slice_fusion.6
  180.8 9.3 %collective-permute-done.2 = bf16[576,384]{1,0:T(8,128)(2,1)S(1)} collective-permute-done((bf16[576,384]{1,0:T(8,128)(2,1)S(1)}, bf16[576,384]{1,0:T(8,128)(2,1)S(1)}, u32[]{:S(2)}, u32[]{:S(2)}) %collective-permute-start.2) | collective-permute-done | bytes 442400 | tf_op jit(solution)/shard_map/ppermute | solution.py:576
  190.7 1.5 collective-permute-start.5
  192.8 2.6 %all-to-all-start.5 = ((f32[32,8,128]{2,1,0:T(8,128)}), f32[32,8,128]{2,1,0:T(8,128)S(1)}, u32[]{:S(2)}, u32[]{:S(2)}) async-start(f32[32,8,128]{2,1,0:T(8,128)} %bitcast.37), calls=%async_computation.5 | async-start | bytes 262144 | tf_op jit(solution)/shard_map/all_to_all | solution.py:45
  196.0 8.5 %all-to-all-done.5 = f32[32,8,128]{2,1,0:T(8,128)S(1)} async-done(((f32[32,8,128]{2,1,0:T(8,128)}), f32[32,8,128]{2,1,0:T(8,128)S(1)}, u32[]{:S(2)}, u32[]{:S(2)}) %all-to-all-start.5) | async-done | bytes 131104 | tf_op jit(solution)/shard_map/all_to_all | solution.py:45
  205.6 2.6 %all-to-all-start.6 = ((f32[32,8,128]{2,1,0:T(8,128)}), f32[32,8,128]{2,1,0:T(8,128)S(1)}, u32[]{:S(2)}, u32[]{:S(2)}) async-start(f32[32,8,128]{2,1,0:T(8,128)} %broadcast_in_dim.106), calls=%async_computation.6 | async-start | bytes 262144 | tf_op jit(solution)/shard_map/all_to_all | solution.py:38
  208.9 1.3 copy.105
  211.8 1.8 collective-permute-start.7
  213.6 1.5 collective-permute-start.6
  215.0 1.5 all-to-all-done.6
  218.0 12.7 %weights.1 = (f32[384,1152]{1,0:T(8,128)}, f32[384,1152]{1,0:T(8,128)}, f32[384,384]{1,0:T(8,128)}, f32[384,384]{1,0:T(8,128)}, f32[384,1536]{1,0:T(8,128)}, /*i...) custom-call(bf16[48,4096]{1,0:T(8,128)(2,1)} %copy-done.6, ...), custom_call_target="tpu_custom_call" | custom-call | tf_op jit(solution)/shard_map/weights/pallas_call | solution.py:795
  232.0 3.1 %collective-permute-done.6.refs_3_ = bf16[2,576,384]{2,1,0:T(8,128)(2,1)} collective-permute-done((bf16[2,576,384]{2,1,0:T(8,128)(2,1)S(1)}, bf16[2,576,384]{2,1,0:T(8,128)(2,1)}, u32[]{:S(2)}, u32[]{:S(2)}) %collective-permute-start.6) | collective-permute-done | bytes 884768 | tf_op jit(solution)/shard_map/ppermute | solution.py:576
  235.1 1.0 copy-done.8
  236.0 8.4 %errors.1 = (f32[384,1152]{1,0:T(8,128)}, f32[384,384]{1,0:T(8,128)}, f32[384,1536]{1,0:T(8,128)}, f32[4,384,384]{2,1,0:T(8,128)}, f32[96,384]{1,0:T(8,128)}) custom-call(s32[1]{0:T(128)} %bitcast.10.me_ref.refs_0_, bf16[48,4096]{1,0:T(8,128)(2,1)} %copy-done.6, bf16[2,576,384]{2,1,0:T(8,128)(2,1)} %copy-done.3, ...), custom_call_target="tpu_custom_call" | custom-call | tf_op jit(solution)/shard_map/errors/pallas_call | solution.py:824
  (95 shorter events, 15.8 us)
Async XLA Ops:
  1.8 19.0 %copy-start.10 = (s32[1,512]{1,0:T(1,128)S(1)}, s32[1,512]{1,0:T(1,128)}, u32[]{:S(2)}) copy-start(s32[1,512]{1,0:T(1,128)} %refs_2_.3) | copy-start | bytes 6148
  1.8 19.9 %copy-start.12 = (s32[64,16]{0,1:T(8,128)S(1)}, s32[64,16]{0,1:T(8,128)}, u32[]{:S(2)}) copy-start(s32[64,16]{0,1:T(8,128)} %param.31) | copy-start | bytes 12292
  1.8 19.9 %copy-start.13 = (s32[64]{0:T(128)S(1)}, s32[64]{0:T(128)}, u32[]{:S(2)}) copy-start(s32[64]{0:T(128)} %param.32) | copy-start | bytes 772
  13.3 25.6 %all-to-all-start = ((bf16[32,64,96]{2,1,0:T(8,128)(2,1)}), bf16[32,64,96]{2,1,0:T(8,128)(2,1)S(1)}, u32[]{:S(2)}, u32[]{:S(2)}) async-start(bf16[32,64,96]{2,1,0:T(8,128)(2,1)} %broadcast_in_dim.94), calls=%async_computation | async-start | bytes 1048576 | tf_op jit(solution)/shard_map/all_to_all | solution.py:38
  22.2 16.6 %copy-start.11 = (s32[1,512]{1,0:T(1,128)S(1)}, s32[1,512]{1,0:T(1,128)}, u32[]{:S(2)}) copy-start(s32[1,512]{1,0:T(1,128)} %refs_2_.3) | copy-start | bytes 6148
  38.8 5.5 %copy-start.5 = (bf16[32,64,96]{2,1,0:T(8,128)(2,1)}, bf16[32,64,96]{2,1,0:T(8,128)(2,1)S(1)}, u32[]{:S(2)}) copy-start(bf16[32,64,96]{2,1,0:T(8,128)(2,1)S(1)} %all-to-all-done) | copy-start | bytes 1179652
  45.8 13.1 %all-to-all-start.1 = ((f32[32,1,256]{2,1,0:T(1,128)}), f32[32,1,256]{2,1,0:T(1,128)S(1)}, u32[]{:S(2)}, u32[]{:S(2)}) async-start(f32[32,1,256]{2,1,0:T(1,128)} %reshape.315), calls=%async_computation.1 | async-start | bytes 65536 | tf_op jit(solution)/shard_map/all_to_all | solution.py:38
  60.9 2.2 copy-start.1
  63.1 1.0 copy-start.9
  65.9 31.5 %all-to-all-start.2 = ((f32[32,64,96]{2,1,0:T(8,128)}), f32[32,64,96]{2,1,0:T(8,128)S(1)}, u32[]{:S(2)}, u32[]{:S(2)}) async-start(f32[32,64,96]{2,1,0:T(8,128)} %bitcast.16), calls=%async_computation.2 | async-start | bytes 2097152 | tf_op jit(solution)/shard_map/all_to_all | solution.py:701
  97.4 1.0 copy-start
  120.7 32.4 %collective-permute-start = (bf16[2,576,384]{2,1,0:T(8,128)(2,1)S(1)}, bf16[2,576,384]{2,1,0:T(8,128)(2,1)}, u32[]{:S(2)}, u32[]{:S(2)}) collective-permute-start(bf16[2,576,384]{2,1,0:T(8,128)(2,1)S(1)} %slice.59), channel_id=1, source_target_pairs={{0,8},{8,0},{16,24},{24,16},{1,9},{9,1},{17,25},{25,17},{2,10},{10... | collective-permute-start | bytes 2654216 | tf_op jit(solution)/shard_map/ppermute | solution.py:576
  123.7 31.1 %collective-permute-start.1 = (bf16[2,608,384]{2,1,0:T(8,128)(2,1)S(1)}, bf16[2,608,384]{2,1,0:T(8,128)(2,1)S(1)}, u32[]{:S(2)}, u32[]{:S(2)}) collective-permute-start(bf16[2,608,384]{2,1,0:T(8,128)(2,1)S(1)} %slice.61), channel_id=1, source_target_pairs={{0,16},{8,24},{16,0},{24,8},{1,17},{9,25},{17,1},{25,9},{2,18},{10... | collective-permute-start | bytes 2801672 | tf_op jit(solution)/shard_map/ppermute | solution.py:576
  125.2 22.4 %all-to-all-start.3 = ((f32[32,8,128]{2,1,0:T(8,128)}), f32[32,8,128]{2,1,0:T(8,128)S(1)}, u32[]{:S(2)}, u32[]{:S(2)}) async-start(f32[32,8,128]{2,1,0:T(8,128)} %bitcast.29), calls=%async_computation.3 | async-start | bytes 262144 | tf_op jit(solution)/shard_map/all_to_all | solution.py:45
  148.3 12.9 %all-to-all-start.4 = ((f32[32,8,128]{2,1,0:T(8,128)}), f32[32,8,128]{2,1,0:T(8,128)S(1)}, u32[]{:S(2)}, u32[]{:S(2)}) async-start(f32[32,8,128]{2,1,0:T(8,128)} %broadcast_in_dim.105), calls=%async_computation.4 | async-start | bytes 262144 | tf_op jit(solution)/shard_map/all_to_all | solution.py:38
  161.2 0.7 copy-start.7
  177.5 17.8 %copy-start.4 = (f32[8,3072]{1,0:T(8,128)S(1)}, f32[8,3072]{1,0:T(8,128)}, u32[]{:S(2)}) copy-start(f32[8,3072]{1,0:T(8,128)} %get-tuple-element.173) | copy-start | bytes 294916
  177.6 13.0 %collective-permute-start.3 = (bf16[608,384]{1,0:T(8,128)(2,1)S(1)}, bf16[608,384]{1,0:T(8,128)(2,1)S(1)}, u32[]{:S(2)}, u32[]{:S(2)}) collective-permute-start(bf16[608,384]{1,0:T(8,128)(2,1)S(1)} %slice_bitcast_fusion), channel_id=1, source_target_pairs={{0,8},{8,0},{16,24},{24,16},{1,9},{9,1},{17,25},{25,17},{2,10},{10... | collective-permute-start | bytes 1400840 | tf_op jit(solution)/shard_map/ppermute | solution.py:576
  178.6 11.6 %collective-permute-start.2 = (bf16[576,384]{1,0:T(8,128)(2,1)S(1)}, bf16[576,384]{1,0:T(8,128)(2,1)S(1)}, u32[]{:S(2)}, u32[]{:S(2)}) collective-permute-start(bf16[576,384]{1,0:T(8,128)(2,1)S(1)} %slice_bitcast_fusion.1), channel_id=1, source_target_pairs={{0,16},{8,24},{16,0},{24,8},{1,17},{9,25},{17,1},{25,9},{2,18},{10... | collective-permute-start | bytes 1327112 | tf_op jit(solution)/shard_map/ppermute | solution.py:576
  190.7 14.0 %collective-permute-start.5 = (bf16[608,384]{1,0:T(8,128)(2,1)S(1)}, bf16[608,384]{1,0:T(8,128)(2,1)S(1)}, u32[]{:S(2)}, u32[]{:S(2)}) collective-permute-start(bf16[608,384]{1,0:T(8,128)(2,1)S(1)} %fusion), channel_id=1, source_target_pairs={{0,8},{8,0},{16,24},{24,16},{1,9},{9,1},{17,25},{25,17},{2,10},{10... | collective-permute-start | bytes 1400840 | tf_op jit(solution)/shard_map/ppermute | solution.py:576
  192.2 12.4 %collective-permute-start.4 = (bf16[576,384]{1,0:T(8,128)(2,1)S(1)}, bf16[576,384]{1,0:T(8,128)(2,1)S(1)}, u32[]{:S(2)}, u32[]{:S(2)}) collective-permute-start(bf16[576,384]{1,0:T(8,128)(2,1)S(1)} %fusion.1), channel_id=1, source_target_pairs={{0,16},{8,24},{16,0},{24,8},{1,17},{9,25},{17,1},{25,9},{2,18},{10... | collective-permute-start | bytes 1327112 | tf_op jit(solution)/shard_map/ppermute | solution.py:576
  192.8 11.8 %all-to-all-start.5 = ((f32[32,8,128]{2,1,0:T(8,128)}), f32[32,8,128]{2,1,0:T(8,128)S(1)}, u32[]{:S(2)}, u32[]{:S(2)}) async-start(f32[32,8,128]{2,1,0:T(8,128)} %bitcast.37), calls=%async_computation.5 | async-start | bytes 262144 | tf_op jit(solution)/shard_map/all_to_all | solution.py:45
  204.7 8.8 %copy-start.3 = (bf16[2,576,384]{2,1,0:T(8,128)(2,1)}, bf16[2,576,384]{2,1,0:T(8,128)(2,1)S(1)}, u32[]{:S(2)}) copy-start(bf16[2,576,384]{2,1,0:T(8,128)(2,1)S(1)} %pad_maximum_fusion.1.refs_2_) | copy-start | bytes 2654212
  204.8 25.9 %copy-start.2 = (bf16[2,608,384]{2,1,0:T(8,128)(2,1)}, bf16[2,608,384]{2,1,0:T(8,128)(2,1)S(1)}, u32[]{:S(2)}) copy-start(bf16[2,608,384]{2,1,0:T(8,128)(2,1)S(1)} %pad_maximum_fusion.refs_4_) | copy-start | bytes 2801668
  205.6 10.9 %all-to-all-start.6 = ((f32[32,8,128]{2,1,0:T(8,128)}), f32[32,8,128]{2,1,0:T(8,128)S(1)}, u32[]{:S(2)}, u32[]{:S(2)}) async-start(f32[32,8,128]{2,1,0:T(8,128)} %broadcast_in_dim.106), calls=%async_computation.6 | async-start | bytes 262144 | tf_op jit(solution)/shard_map/all_to_all | solution.py:38
  211.8 23.3 %collective-permute-start.7 = (bf16[2,608,384]{2,1,0:T(8,128)(2,1)S(1)}, bf16[2,608,384]{2,1,0:T(8,128)(2,1)S(1)}, u32[]{:S(2)}, u32[]{:S(2)}) collective-permute-start(bf16[2,608,384]{2,1,0:T(8,128)(2,1)S(1)} %pad_maximum_fusion.refs_4_), channel_id=1, source_target_pairs={{0,16},{8,24},{16,0},{24,8},{1,17},{9,25},{17,1},{25,9},{2,18},{10... | collective-permute-start | bytes 2801672 | tf_op jit(solution)/shard_map/ppermute | solution.py:576
  213.6 21.5 %collective-permute-start.6 = (bf16[2,576,384]{2,1,0:T(8,128)(2,1)S(1)}, bf16[2,576,384]{2,1,0:T(8,128)(2,1)}, u32[]{:S(2)}, u32[]{:S(2)}) collective-permute-start(bf16[2,576,384]{2,1,0:T(8,128)(2,1)S(1)} %pad_maximum_fusion.1.refs_2_), channel_id=1, source_target_pairs={{0,8},{8,0},{16,24},{24,16},{1,9},{9,1},{17,25},{25,17},{2,10},{10... | collective-permute-start | bytes 2654216 | tf_op jit(solution)/shard_map/ppermute | solution.py:576
  217.3 0.8 copy-start.6
  235.1 1.0 copy-start.8
